TPU v7x, 128 devices: a whole 4x4x4 slice. The times are simulated.
128 devices in a mesh: ep: 4 (over z), tm: 32 (over y, x, core).
Axes of the slice: x: 4, y: 4, z: 4, core: 2. Of those that a mesh axis runs over, the one named last changes fastest.
Arguments:
- states: bfloat16 [24, 4096, 1024], P('ep', 'tm'), may hold values from -26 to 26
- norm_gain: float32 [1024], replicated, may hold values from 0.25 to 4
- w_query: bfloat16 [1024, 1024], replicated, may hold values from -0.1875 to 0.1875
- w_keyval: bfloat16 [1024, 2048], replicated, may hold values from -0.1875 to 0.1875
- w_out: bfloat16 [1024, 1024], replicated, may hold values from -0.1875 to 0.1875
- rel_bias: float32 [8, 256], replicated, may hold values from -2.5 to 160
- w_policy: bfloat16 [1024, 128], replicated, may hold values from -8.125 to 8.125
- w_value: bfloat16 [1024], replicated, may hold values from -0.1875 to 0.1875
- actions: int32 [24, 4096], P('ep', 'tm'), may hold values from 0 to 127
- legal_mask: int32 [24, 4096, 128], P('ep', 'tm'), may hold values from 0 to 1, as said below
- rewards: int32 [24, 4096], P('ep', 'tm'), may hold values from -1 to 1
- episode_end: int32 [24, 4096], P('ep', 'tm'), may hold values from 0 to 1
- behavior_logprob: float32 [24, 4096], P('ep', 'tm'), may hold values from -8 to 0
- reg_logprob: float32 [24, 4096], P('ep', 'tm'), may hold values from -8 to 0
Outputs:
- grads: float32 [1024, 4224], P(('ep', 'tm'))
Inputs may be any that keep to these rules, and one draw needn't show every extreme that they name: legal_mask is 1 at the sampled action of every step.
All inputs are finite; a program needn't handle non-finite values.
Results may differ from a plain program's by a relative error of at most 0.012.
Values may be sent and summed in bfloat16 or wider, within the bound.
No kernel may reach another device: no remote copies, remote signals or barrier semaphores. Data moves between devices by JAX's collectives and lax.ppermute only.
A program may use at most 128 MiB of HBM per device.

v0:
```python
import functools
import math

import jax
import jax.numpy as jnp
from jax import lax
from jax.experimental import pallas as pl
from jax.experimental.pallas import tpu as pltpu
from jax.sharding import Mesh
from jax.sharding import PartitionSpec as P


norm_eps = 1e-06
grad_eps = 1e-06
reg_weight = 0.2
adv_clip = 20.0
masked_score = -1e30
EVERY = ("z", "y", "x", "c")
TIME = ("y", "x", "c")


EPS = 6
LEN = 128
ROWS = EPS * LEN
WIDTH = 1024
HEAD = 128
PAIR = 2 * HEAD
HALF = 4 * HEAD
ACTS = 128
SEGS = 32
score_scale = 1.0 / math.sqrt(HEAD)
VMEM_LIMIT = 67_043_328

f32 = jnp.float32
bf16 = jnp.bfloat16


def dot(left, right, left_dim, right_dim):
    return lax.dot_general(
        left, right, (((left_dim,), (right_dim,)), ((), ())), preferred_element_type=f32
    )


def rms_norm(states, norm_gain):
    widened = states.astype(f32)
    spread = jnp.mean(widened * widened, axis=-1, keepdims=True)
    return (widened * lax.rsqrt(spread + norm_eps) * norm_gain).astype(bf16)


def full(shape):
    return pl.BlockSpec(shape, lambda *_: (0,) * len(shape))


def params():
    return pltpu.CompilerParams(
        dimension_semantics=("arbitrary",), vmem_limit_bytes=VMEM_LIMIT
    )


def project_kernel(states_ref, gain_ref, wq_ref, wkv_ref, out_ref, turned_ref, normed_ref):
    step = pl.program_id(0)

    @pl.when(step == 0)
    def _():
        for e in range(EPS):
            rows = pl.ds(e * LEN, LEN)
            normed = rms_norm(states_ref[rows, :], gain_ref[...])
            normed_ref[rows, :] = normed
            turned_ref[:, rows] = normed.T

    @pl.when(step < 2)
    def _():
        out_ref[...] = dot(normed_ref[...], wq_ref[...], 1, 0).astype(bf16)

    @pl.when(step >= 2)
    def _():
        out_ref[...] = dot(normed_ref[...], wkv_ref[...], 1, 0).astype(bf16)


def project(states, gain, w_query, w_keyval):
    return pl.pallas_call(
        project_kernel,
        grid=(6,),
        in_specs=[
            full((ROWS, WIDTH)),
            full((1, WIDTH)),
            pl.BlockSpec((WIDTH, 512), lambda j: (0, jnp.minimum(j, 1))),
            pl.BlockSpec((WIDTH, 512), lambda j: (0, jnp.maximum(j - 2, 0))),
        ],
        out_specs=[
            pl.BlockSpec((ROWS, 512), lambda j: (0, j)),
            full((WIDTH, ROWS)),
        ],
        out_shape=[
            jax.ShapeDtypeStruct((ROWS, 3 * WIDTH), bf16),
            jax.ShapeDtypeStruct((WIDTH, ROWS), bf16),
        ],
        scratch_shapes=[pltpu.VMEM((ROWS, WIDTH), bf16)],
        compiler_params=params(),
        cost_estimate=pl.CostEstimate(
            flops=2 * ROWS * WIDTH * 3 * WIDTH, bytes_accessed=14_000_000, transcendentals=0
        ),
        name="project",
    )(states, gain, w_query, w_keyval)


def action_masks(legal_ref, actions_ref, block, e):
    legal = legal_ref[block].astype(f32).T > 0.0
    chosen = lax.broadcasted_iota(jnp.int32, (ACTS, LEN), 0) == actions_ref[e : e + 1, :]
    return legal, chosen


def by_head(rows):
    zeros = jnp.zeros((LEN, HEAD), rows.dtype)
    upper = jnp.concatenate([rows[:, :HEAD], zeros], axis=1)
    lower = jnp.concatenate([zeros, rows[:, HEAD:]], axis=1)
    return jnp.concatenate([upper, lower], axis=0)


def suffix_scan(decay, *sums):
    lane = lax.broadcasted_iota(jnp.int32, decay.shape, 1)
    reach = 1
    while reach < LEN:
        inside = lane < LEN - reach
        ahead = [
            jnp.where(inside, pltpu.roll(part, LEN - reach, 1), 0.0) for part in sums
        ]
        sums = [part + decay * after for part, after in zip(sums, ahead)]
        decay = decay * jnp.where(inside, pltpu.roll(decay, LEN - reach, 1), 1.0)
        reach *= 2
    return (decay, *sums)


def pad_rows(part):
    return jnp.concatenate([part, jnp.zeros((8 - part.shape[0], LEN), f32)], axis=0)


def attend_kernel(
    has_ref,
    mem_ref,
    gain_ref,
    wk_ref,
    wv_ref,
    q_ref,
    kc_ref,
    vc_ref,
    bias_ref,
    wout_ref,
    states_hbm,
    wpolicy_ref,
    wvalue_ref,
    legal_hbm,
    actions_ref,
    rewards_ref,
    ends_ref,
    behavior_ref,
    reg_ref,
    turned_hbm,
    kmem_ref,
    vmem_ref,
    probs_ref,
    attt_ref,
    hidden_hbm,
    stats_ref,
    told_ref,
    memn_ref,
    acc_ref,
    att_ref,
    states_ref,
    legal_ref,
    turned_ref,
    hidden_ref,
    sem_ref,
):
    step = pl.program_id(0)
    states_copy = pltpu.make_async_copy(states_hbm, states_ref, sem_ref.at[0])
    legal_copy = pltpu.make_async_copy(legal_hbm, legal_ref, sem_ref.at[1])
    turned_copy = pltpu.make_async_copy(turned_ref, turned_hbm, sem_ref.at[2])
    hidden_copy = pltpu.make_async_copy(hidden_ref, hidden_hbm, sem_ref.at[3])

    @pl.when(step == 0)
    def _():
        for e in range(EPS):
            rows = pl.ds(e * LEN, LEN)
            normed = rms_norm(mem_ref[rows, :], gain_ref[...])
            memn_ref[rows, :] = normed
            turned_ref[:, rows] = normed.T
        states_copy.start()
        legal_copy.start()
        turned_copy.start()

    kmem_ref[...] = dot(memn_ref[...], wk_ref[...], 1, 0).astype(bf16)
    vmem_ref[...] = dot(memn_ref[...], wv_ref[...], 1, 0).astype(bf16)

    key_index = lax.broadcasted_iota(jnp.int32, (2 * LEN, LEN), 0)
    query_index = lax.broadcasted_iota(jnp.int32, (2 * LEN, LEN), 1)
    reach = jnp.where(key_index < LEN, LEN * has_ref[0] - 1, LEN + query_index)
    allowed = key_index <= reach
    grids = []
    for h in range(2):
        line = bias_ref[pl.ds(2 * step + h, 1), :]
        grid = pltpu.roll(
            jnp.broadcast_to(line, (2 * LEN, 2 * LEN)), LEN, 1, stride=1, stride_axis=0
        )
        grids.append(grid[:, :LEN])

    for e in range(EPS):
        rows = pl.ds(e * LEN, LEN)
        both = pl.ds(2 * e * LEN, 2 * LEN)
        keys = jnp.concatenate([kmem_ref[rows, :], kc_ref[rows, :]], axis=0)
        values = jnp.concatenate([vmem_ref[rows, :], vc_ref[rows, :]], axis=0)
        products = dot(keys, by_head(q_ref[rows, :]), 1, 1)
        for h in range(2):
            cols = pl.ds(h * HEAD, HEAD)
            scores = products[:, h * LEN : (h + 1) * LEN]
            scores = jnp.where(allowed, scores * score_scale + grids[h], masked_score)
            highest = jnp.max(scores, axis=0, keepdims=True)
            weights = jnp.exp(scores - highest)
            weights = weights * (1.0 / jnp.sum(weights, axis=0, keepdims=True))
            weights = weights.astype(bf16)
            probs_ref[both, cols] = weights
            mixed = dot(weights, values[:, h * HEAD : (h + 1) * HEAD], 0, 0)
            att_ref[rows, cols] = mixed.astype(bf16)

    attt_ref[...] = att_ref[...].T
    part = dot(att_ref[...], wout_ref[...], 1, 0)

    @pl.when(step == 0)
    def _():
        acc_ref[...] = part

    @pl.when(step > 0)
    def _():
        acc_ref[...] += part

    @pl.when(step == 3)
    def _():
        states_copy.wait()
        hidden = (states_ref[...].astype(f32) + acc_ref[...]).astype(bf16)
        hidden_ref[...] = hidden
        hidden_copy.start()
        legal_copy.wait()
        all_logits = dot(wpolicy_ref[...].T, hidden, 1, 1)
        all_values = dot(jnp.broadcast_to(wvalue_ref[...], (16, WIDTH)), hidden, 1, 1)
        log_rows, value_rows = [], []
        for e in range(EPS):
            logits = all_logits[:, e * LEN : (e + 1) * LEN]
            legal, chosen = action_masks(legal_ref, actions_ref, e, e)
            highest = jnp.max(jnp.where(legal, logits, masked_score), axis=0, keepdims=True)
            partition = jnp.sum(
                jnp.where(legal, jnp.exp(jnp.where(legal, logits - highest, 0.0)), 0.0),
                axis=0,
                keepdims=True,
            )
            picked = jnp.sum(jnp.where(chosen, logits, 0.0), axis=0, keepdims=True)
            log_rows.append(picked - highest - jnp.log(partition))
            value_rows.append(all_values[0:1, e * LEN : (e + 1) * LEN])
        log_taken = jnp.concatenate(log_rows, axis=0)
        values = jnp.concatenate(value_rows, axis=0)
        clipped = jnp.minimum(1.0, jnp.exp(log_taken - behavior_ref[...]))
        shaped = rewards_ref[...].astype(f32) - reg_weight * (log_taken - reg_ref[...])
        carry_on = 1.0 - ends_ref[...].astype(f32)
        last = lax.broadcasted_iota(jnp.int32, (EPS, LEN), 1) == LEN - 1
        next_local = jnp.where(last, 0.0, pltpu.roll(values, LEN - 1, 1))
        td_error = clipped * (shaped + carry_on * next_local - values)
        decay = carry_on * clipped
        bridge = jnp.where(last, decay, 0.0)
        kept = [*suffix_scan(decay, td_error, bridge), values, log_taken]
        kept = [pad_rows(part) for part in kept]
        for index, part in enumerate(kept):
            stats_ref[index] = part
        stacked = jnp.concatenate(kept[:4] + [jnp.zeros((LEN - 32, LEN), f32)], axis=0)
        told_ref[...] = jnp.broadcast_to(stacked.T[0:1, :], (SEGS, LEN))
        turned_copy.wait()
        hidden_copy.wait()


def attend(has_memory, mem_states, gain, w_keyval, qkv, weights, states, steps):
    w_out, rel_bias, w_policy, w_value = weights
    legal_mask, actions, rewards, ends, behavior, reg = steps
    small = full((EPS, LEN))
    inputs = [
        has_memory,
        mem_states,
        gain,
        w_keyval,
        w_keyval,
        qkv,
        qkv,
        qkv,
        rel_bias,
        w_out,
        states,
        w_policy,
        w_value,
        legal_mask,
        actions,
        rewards,
        ends,
        behavior,
        reg,
    ]
    in_specs = [
        pl.BlockSpec(memory_space=pltpu.SMEM),
        full((ROWS, WIDTH)),
        full((1, WIDTH)),
        pl.BlockSpec((WIDTH, PAIR), lambda g: (0, g)),
        pl.BlockSpec((WIDTH, PAIR), lambda g: (0, 4 + g)),
        pl.BlockSpec((ROWS, PAIR), lambda g: (0, g)),
        pl.BlockSpec((ROWS, PAIR), lambda g: (0, 4 + g)),
        pl.BlockSpec((ROWS, PAIR), lambda g: (0, 8 + g)),
        full((8, 2 * LEN)),
        pl.BlockSpec((PAIR, WIDTH), lambda g: (g, 0)),
        pl.BlockSpec(memory_space=pl.ANY),
        full((WIDTH, ACTS)),
        full((1, WIDTH)),
        pl.BlockSpec(memory_space=pl.ANY),
        small,
        small,
        small,
        small,
        small,
    ]
    out_specs = [
        pl.BlockSpec(memory_space=pl.ANY),
        pl.BlockSpec((ROWS, PAIR), lambda g: (0, g)),
        pl.BlockSpec((ROWS, PAIR), lambda g: (0, g)),
        pl.BlockSpec((2 * ROWS, PAIR), lambda g: (0, g)),
        pl.BlockSpec((PAIR, ROWS), lambda g: (g, 0)),
        pl.BlockSpec(memory_space=pl.ANY),
        full((5, 8, LEN)),
        full((SEGS, LEN)),
    ]
    out_shape = [
        jax.ShapeDtypeStruct((WIDTH, ROWS), bf16),
        jax.ShapeDtypeStruct((ROWS, WIDTH), bf16),
        jax.ShapeDtypeStruct((ROWS, WIDTH), bf16),
        jax.ShapeDtypeStruct((2 * ROWS, WIDTH), bf16),
        jax.ShapeDtypeStruct((WIDTH, ROWS), bf16),
        jax.ShapeDtypeStruct((ROWS, WIDTH), bf16),
        jax.ShapeDtypeStruct((5, 8, LEN), f32),
        jax.ShapeDtypeStruct((SEGS, LEN), f32),
    ]
    return pl.pallas_call(
        attend_kernel,
        grid=(4,),
        in_specs=in_specs,
        out_specs=out_specs,
        out_shape=out_shape,
        scratch_shapes=[
            pltpu.VMEM((ROWS, WIDTH), bf16),
            pltpu.VMEM((ROWS, WIDTH), f32),
            pltpu.VMEM((ROWS, PAIR), bf16),
            pltpu.VMEM((ROWS, WIDTH), bf16),
            pltpu.VMEM((EPS, LEN, ACTS), jnp.int32),
            pltpu.VMEM((WIDTH, ROWS), bf16),
            pltpu.VMEM((ROWS, WIDTH), bf16),
            pltpu.SemaphoreType.DMA((4,)),
        ],
        compiler_params=params(),
        cost_estimate=pl.CostEstimate(
            flops=4_000_000_000, bytes_accessed=15_000_000, transcendentals=800_000
        ),
        name="attend",
    )(*inputs)


def cotangent_kernel(
    me_ref,
    told_ref,
    stats_ref,
    rewards_ref,
    ends_ref,
    behavior_ref,
    reg_ref,
    legal_ref,
    actions_ref,
    wpolicy_ref,
    wvalue_ref,
    hidden_ref,
    wout_ref,
    attt_ref,
    attcot_ref,
    own_ref,
    other_ref,
    gpol_ref,
    hcot_ref,
    lcot_ref,
):
    step = pl.program_id(0)

    @pl.when(step == 0)
    def _():
        told = told_ref[...]
        delta, bridge, first = [pltpu.roll(told, LEN - 8 * n, 1) for n in (1, 2, 3)]
        me = me_ref[0]
        incoming = jnp.zeros((1, LEN), f32)
        next_value = jnp.zeros((1, LEN), f32)
        for seg in range(SEGS - 1, 0, -1):
            row = slice(seg, seg + 1)
            gap = delta[row] + bridge[row] * next_value + told[row] * incoming
            incoming = jnp.where(seg > me, gap, incoming)
            next_value = jnp.where(seg > me, first[row], next_value)
        incoming = jnp.broadcast_to(incoming, (LEN, LEN)).T[:EPS]
        next_value = jnp.broadcast_to(next_value, (LEN, LEN)).T[:EPS]

        acc_decay, acc_delta, acc_bridge, values, log_taken = [
            stats_ref[index][:EPS] for index in range(5)
        ]
        behavior = behavior_ref[...]
        shaped = rewards_ref[...].astype(f32) - reg_weight * (log_taken - reg_ref[...])
        carry_on = 1.0 - ends_ref[...].astype(f32)
        target_gap = acc_delta + acc_bridge * next_value + acc_decay * incoming
        targets = values + target_gap
        last = lax.broadcasted_iota(jnp.int32, (EPS, LEN), 1) == LEN - 1
        next_targets = jnp.where(last, next_value + incoming, pltpu.roll(targets, LEN - 1, 1))
        spread = (shaped + carry_on * next_targets - values) * jnp.exp(-behavior)
        taken_prob = jnp.exp(log_taken)
        adv_taken = jnp.clip((1.0 - taken_prob) * spread, -adv_clip, adv_clip)
        adv_other = jnp.clip(-taken_prob * spread, -adv_clip, adv_clip)
        value_cot = jnp.concatenate(
            [values - targets, jnp.zeros((LEN - EPS, LEN), f32)], axis=0
        ).T
        w_policy = wpolicy_ref[...].T
        w_value = wvalue_ref[...].astype(f32)
        for e in range(EPS):
            legal, chosen = action_masks(legal_ref, actions_ref, e, e)
            advantage = jnp.where(chosen, adv_taken[e : e + 1], adv_other[e : e + 1])
            logit_cot = jnp.where(legal, -advantage, 0.0)
            lcot_ref[:, pl.ds(e * LEN, LEN)] = logit_cot.astype(bf16)
            cot = dot(logit_cot.T.astype(bf16), w_policy, 1, 0)
            cot = cot + value_cot[:, e : e + 1] * w_value
            hcot_ref[pl.ds(e * LEN, LEN), :] = cot.astype(bf16)
        gpol_ref[...] = dot(lcot_ref[...], hidden_ref[...], 1, 0).T.astype(bf16)

    attcot_ref[...] = dot(hcot_ref[...], wout_ref[...], 1, 1).astype(bf16)
    core = lax.rem(me_ref[0], 2)
    for half, grad_ref in ((core, own_ref), (1 - core, other_ref)):
        cols = pl.ds(pl.multiple_of(half * HALF, HALF), HALF)
        grad_ref[...] = dot(attt_ref[...], hcot_ref[:, cols], 1, 0).astype(bf16)


def cotangents(me, told, stats, steps, weights, hidden, attended_turned):
    w_out, _, w_policy, w_value = weights
    legal_mask, actions, rewards, ends, behavior, reg = steps
    small = full((EPS, LEN))
    return pl.pallas_call(
        cotangent_kernel,
        grid=(4,),
        in_specs=[
            pl.BlockSpec(memory_space=pltpu.SMEM),
            full((SEGS, LEN)),
            full((5, 8, LEN)),
            small,
            small,
            small,
            small,
            full((EPS, LEN, ACTS)),
            small,
            full((WIDTH, ACTS)),
            full((1, WIDTH)),
            full((ROWS, WIDTH)),
            pl.BlockSpec((PAIR, WIDTH), lambda n: (n, 0)),
            pl.BlockSpec((PAIR, ROWS), lambda n: (n, 0)),
        ],
        out_specs=[
            pl.BlockSpec((ROWS, PAIR), lambda n: (0, n)),
            pl.BlockSpec((PAIR, HALF), lambda n: (n, 0)),
            pl.BlockSpec((PAIR, HALF), lambda n: (n, 0)),
            full((WIDTH, ACTS)),
        ],
        out_shape=[
            jax.ShapeDtypeStruct((ROWS, WIDTH), bf16),
            jax.ShapeDtypeStruct((WIDTH, HALF), bf16),
            jax.ShapeDtypeStruct((WIDTH, HALF), bf16),
            jax.ShapeDtypeStruct((WIDTH, ACTS), bf16),
        ],
        scratch_shapes=[
            pltpu.VMEM((ROWS, WIDTH), bf16),
            pltpu.VMEM((ACTS, ROWS), bf16),
        ],
        compiler_params=params(),
        cost_estimate=pl.CostEstimate(
            flops=4_000_000_000, bytes_accessed=12_000_000, transcendentals=10_000
        ),
        name="cotangents",
    )(
        me,
        told,
        stats,
        rewards,
        ends,
        behavior,
        reg,
        legal_mask,
        actions,
        w_policy,
        w_value,
        hidden,
        w_out,
        attended_turned,
    )


def heads_kernel(
    first_ref,
    cot_ref,
    probs_ref,
    q_ref,
    kmem_ref,
    kc_ref,
    vmem_ref,
    vc_ref,
    turned_ref,
    memt_ref,
    grad_ref,
    new_ref,
    old_ref,
):
    for e in range(EPS):
        rows, both = pl.ds(e * LEN, LEN), pl.ds(2 * e * LEN, 2 * LEN)
        cot = by_head(cot_ref[rows, :])
        weights = probs_ref[both, :]
        wide = weights.astype(f32)
        keys = jnp.concatenate([kmem_ref[rows, :], kc_ref[rows, :]], axis=0)
        values = jnp.concatenate([vmem_ref[rows, :], vc_ref[rows, :]], axis=0)
        weight_cot = dot(values, cot, 1, 1).astype(bf16).astype(f32)
        product = wide * weight_cot
        inner = jnp.sum(product, axis=0, keepdims=True)
        score_cot = ((product - wide * inner) * score_scale).astype(bf16)
        value_grad = dot(weights, cot, 1, 0).astype(bf16)
        key_grad = dot(score_cot, by_head(q_ref[rows, :]), 1, 0).astype(bf16)
        for h in range(2):
            cols = pl.ds(h * HEAD, HEAD)
            new_ref[rows, cols] = dot(
                score_cot[:, h * LEN : (h + 1) * LEN],
                keys[:, h * HEAD : (h + 1) * HEAD],
                0,
                0,
            ).astype(bf16)
        new_ref[rows, pl.ds(PAIR, PAIR)] = key_grad[LEN:]
        new_ref[rows, pl.ds(2 * PAIR, PAIR)] = value_grad[LEN:]
        old_ref[rows, pl.ds(0, PAIR)] = key_grad[:LEN]
        old_ref[rows, pl.ds(PAIR, PAIR)] = value_grad[:LEN]
    for half in range(2):
        part = pl.ds(half * 512, 512)
        fresh = dot(turned_ref[part, :], new_ref[...], 1, 0)
        stale = dot(memt_ref[part, :], old_ref[...], 1, 0)
        grad_ref[part, pl.ds(0, PAIR)] = fresh[:, :PAIR].astype(bf16)
        grad_ref[part, pl.ds(PAIR, 2 * PAIR)] = (fresh[:, PAIR:] + stale).astype(bf16)


def heads_backward(first, att_cot, probs, qkv, kmem, vmem, turned, mem_turned):
    return pl.pallas_call(
        heads_kernel,
        grid_spec=pltpu.PrefetchScalarGridSpec(
            num_scalar_prefetch=1,
            grid=(2,),
            in_specs=[
                pl.BlockSpec((ROWS, PAIR), lambda g, first: (0, first[0] + g)),
                pl.BlockSpec((2 * ROWS, PAIR), lambda g, first: (0, first[0] + g)),
                pl.BlockSpec((ROWS, PAIR), lambda g, first: (0, first[0] + g)),
                pl.BlockSpec((ROWS, PAIR), lambda g, first: (0, first[0] + g)),
                pl.BlockSpec((ROWS, PAIR), lambda g, first: (0, 4 + first[0] + g)),
                pl.BlockSpec((ROWS, PAIR), lambda g, first: (0, first[0] + g)),
                pl.BlockSpec((ROWS, PAIR), lambda g, first: (0, 8 + first[0] + g)),
                full((WIDTH, ROWS)),
                full((WIDTH, ROWS)),
            ],
            out_specs=pl.BlockSpec((WIDTH, 3 * PAIR), lambda g, first: (0, g)),
            scratch_shapes=[
                pltpu.VMEM((ROWS, 3 * PAIR), bf16),
                pltpu.VMEM((ROWS, 2 * PAIR), bf16),
            ],
        ),
        out_shape=jax.ShapeDtypeStruct((WIDTH, 6 * PAIR), bf16),
        compiler_params=params(),
        cost_estimate=pl.CostEstimate(
            flops=5_000_000_000, bytes_accessed=14_000_000, transcendentals=0
        ),
        name="heads_backward",
    )(first, att_cot, probs, qkv, kmem, qkv, vmem, qkv, turned, mem_turned)


COLS_C = HALF + ACTS


def pair_kernel(place_ref, own_ref, got_ref, oown_ref, ogot_ref, pol_ref, *out_refs):
    a_refs, b_refs, c_refs = out_refs[:4], out_refs[4:8], out_refs[8:]
    step = pl.program_id(0)

    def paired(index, cols):
        left = own_ref[0, index, :, :, cols].astype(f32)
        return (left + got_ref[0, index, :, :, cols].astype(f32)).astype(bf16)

    def paired_out(index, cols):
        left = oown_ref[0, index, :, :, cols].astype(f32)
        return (left + ogot_ref[0, index, :, :, cols].astype(f32)).astype(bf16)

    for j in range(4):
        x = lax.rem(place_ref[0] + j, 4)
        y = lax.rem(place_ref[1] + j, 4)
        for p in range(4):
            for n, half in enumerate((pl.ds(0, PAIR), pl.ds(3 * PAIR, PAIR))):
                value = own_ref[0, p, x, :, half].astype(f32) + got_ref[0, p, x, :, half].astype(f32)
                a_refs[j][0, p, :, pl.ds(n * PAIR, PAIR)] = value.astype(bf16)
            half = pl.ds(0, PAIR)
            value = oown_ref[0, p, x, :, half].astype(f32) + ogot_ref[0, p, x, :, half].astype(f32)
            a_refs[j][0, p, :, pl.ds(2 * PAIR, PAIR)] = value.astype(bf16)
        for n in range(2):
            b_refs[j][0, :, :, pl.ds(n * PAIR, PAIR)] = paired(y, pl.ds((3 * n + 1) * PAIR, PAIR))
        b_refs[j][0, :, :, pl.ds(2 * PAIR, PAIR)] = paired_out(y, pl.ds(PAIR, PAIR))

        @pl.when(step == j)
        def _(j=j):
            for p in range(4):
                for n in range(2):
                    c_refs[j][p, :, :, pl.ds(n * PAIR, PAIR)] = paired(
                        p, pl.ds((3 * n + 2) * PAIR, PAIR)
                    )
                c_refs[j][p, :, :, pl.ds(HALF, ACTS)] = pol_ref[0, p]


def pair_sum(place, own, got, out_own, out_got, policy):
    def layer(cols):
        return pl.BlockSpec(
            (1, 4, 4, 16, cols), lambda j, place: (lax.rem(place[2] + j, 4), 0, 0, 0, 0)
        )

    group = pl.BlockSpec((1, 4, 16, 768), lambda j, place: (lax.rem(place[2] + j, 4), 0, 0, 0))
    last = pl.BlockSpec((4, 4, 16, COLS_C), lambda j, place: (0, 0, 0, 0))
    parts = [part.reshape(4, 4, 4, 16, -1) for part in (own, got, out_own, out_got, policy)]
    shapes = [jax.ShapeDtypeStruct((4, 4, 16, 768), bf16)] * 8
    shapes += [jax.ShapeDtypeStruct((4, 4, 16, COLS_C), bf16)] * 4
    out = pl.pallas_call(
        pair_kernel,
        grid_spec=pltpu.PrefetchScalarGridSpec(
            num_scalar_prefetch=1,
            grid=(4,),
            in_specs=[layer(part.shape[-1]) for part in parts],
            out_specs=[group] * 8 + [last] * 4,
        ),
        out_shape=shapes,
        compiler_params=params(),
        name="pair_sum",
    )(place, *parts)
    return out[:4], out[4:8], out[8:]


def ring(count, step):
    return [(source, (source + step) % count) for source in range(count)]


def swapped(part):
    return lax.ppermute(part, "c", ring(2, 1))


def hop_sum(blocks, axis):
    total = blocks[0].astype(f32)
    for step in (2, 1, 3):
        got = lax.ppermute(blocks[step].astype(bf16), axis, ring(4, step))
        total = total + got.astype(f32)
    return total


def further(total, position, axis):
    mine = lax.axis_index(axis)
    return [
        lax.dynamic_index_in_dim(total, (mine + step) % 4, position, keepdims=False)
        for step in range(4)
    ]


def sum_over_devices(own, got, out_own, out_got, policy):
    core = lax.axis_index("c")
    place = jnp.stack([lax.axis_index(axis) for axis in "xyz"])
    a_blocks, b_blocks, c_blocks = pair_sum(place, own, got, out_own, out_got, policy)
    a = hop_sum(a_blocks, "x")
    b = hop_sum(b_blocks, "y")
    c = hop_sum(c_blocks, "z")
    ac = [
        jnp.concatenate([left.astype(bf16), right.astype(bf16)], axis=2)
        for left, right in zip(further(a, 1, "y"), further(c, 0, "y"))
    ]
    ac = hop_sum(ac, "y")
    b = hop_sum(further(b, 1, "x"), "x")
    ab = jnp.concatenate([ac[:, :, :768], b], axis=2).astype(bf16).reshape(8, 8, 1536)
    ab = lax.all_to_all(ab, ("z", "c"), 0, 0, tiled=True).reshape(4, 2, 8, 1536)
    ab = jnp.sum(ab.astype(f32), axis=0)
    c = hop_sum(further(ac[:, :, 768:], 0, "x"), "x").reshape(2, 8, COLS_C)
    mine = lax.dynamic_index_in_dim(c, core, 0, keepdims=False)
    theirs = swapped(lax.dynamic_index_in_dim(c, 1 - core, 0, keepdims=False))
    c = jnp.stack([jnp.where(core == 0, mine, theirs), jnp.where(core == 0, theirs, mine)])
    out = jnp.concatenate([ab[:, :, 512:768], ab[:, :, 1280:]], axis=2)
    square = [ab[:, :, :512], ab[:, :, 768:1280], c[:, :, :HALF], out]
    columns = [part.transpose(1, 0, 2).reshape(8, WIDTH) for part in square]
    return jnp.concatenate([*columns, c[0, :, HALF:] + c[1, :, HALF:]], axis=1)


def body(
    states,
    norm_gain,
    w_query,
    w_keyval,
    w_out,
    rel_bias,
    w_policy,
    w_value,
    actions,
    legal_mask,
    rewards,
    episode_end,
    behavior_logprob,
    reg_logprob,
):
    core, segment = lax.axis_index("c"), lax.axis_index(TIME)
    states = states.reshape(ROWS, WIDTH)
    links = [(source, source + 1) for source in range(SEGS - 1)]
    mem_states = lax.ppermute(states, TIME, links)
    gain = norm_gain.reshape(1, WIDTH)
    steps = (legal_mask, actions, rewards, episode_end, behavior_logprob, reg_logprob)
    weights = (w_out, rel_bias, w_policy, w_value.reshape(1, WIDTH))

    qkv, turned = project(states, gain, w_query, w_keyval)
    has_memory = (segment > 0).astype(jnp.int32).reshape(1)
    mem_turned, kmem, vmem, probs, att_turned, hidden, stats, told = attend(
        has_memory, mem_states, gain, w_keyval, qkv, weights, states, steps
    )
    told = lax.all_to_all(told, TIME, 0, 0, tiled=True)
    att_cot, out_own, out_other, grad_policy = cotangents(
        segment.reshape(1), told, stats, steps, weights, hidden, att_turned
    )
    out_got = swapped(out_other)
    backward = functools.partial(
        heads_backward,
        att_cot=att_cot,
        probs=probs,
        qkv=qkv,
        kmem=kmem,
        vmem=vmem,
        turned=turned,
        mem_turned=mem_turned,
    )
    got = swapped(backward(first=(2 * (1 - core)).reshape(1)))
    owned = backward(first=(2 * core).reshape(1))
    raw_rows = sum_over_devices(owned, got, out_own, out_got, grad_policy)
    squares = jnp.sum(raw_rows * raw_rows)
    spread = jnp.broadcast_to(squares * (1.0 / 128.0), (128, 128))
    grand_total = jnp.sum(lax.all_to_all(spread, EVERY, 0, 0, tiled=True))
    entry_count = WIDTH * raw_rows.shape[1]
    clip_scale = jnp.minimum(1.0, math.sqrt(entry_count) / jnp.sqrt(grand_total + grad_eps))
    return raw_rows * clip_scale


def solution(mesh):
    fine = Mesh(mesh.devices.reshape(4, 4, 4, 2), EVERY)
    by_step = P("z", TIME)
    return jax.shard_map(
        body,
        mesh=fine,
        in_specs=(
            P("z", TIME, None),
            P(),
            P(),
            P(),
            P(),
            P(),
            P(),
            P(),
            by_step,
            P("z", TIME, None),
            by_step,
            by_step,
            by_step,
            by_step,
        ),
        out_specs=P(EVERY, None),
        check_vma=False,
    )
```

profile of v0, /device:TPU:1, one launch (start us, length us, event | category | flops | bytes accessed | tf_op | source)
XLA Modules:
  0.0 185.3 jit_solution(4026913139950515891)
XLA Ops:
  0.0 4.5 %collective-permute-start = (bf16[768,1024]{1,0:T(8,128)(2,1)}, bf16[768,1024]{1,0:T(8,128)(2,1)}, u32[]{:S(2)}, u32[]{:S(2)}) collective-permute-start(bf16[768,1024]{1,0:T(8,128)(2,1)} %bitcast.119), channel_id=1, source_target_pairs={{0,1},{1,2},{2,3},{3,4},{4,5},{5,6},{6,7},{7,8},{8,9},{9,10},{10,1... | collective-permute-start | bytes 4718600 | tf_op jit(solution)/shard_map/ppermute | solution.py:719
  4.5 1.3 reshape.86.wvalue_ref
  5.8 11.4 %project.1 = (bf16[768,3072]{1,0:T(8,128)(2,1)}, bf16[1024,768]{1,0:T(8,128)(2,1)}) custom-call(bf16[768,1024]{1,0:T(8,128)(2,1)} %bitcast.120, f32[1,1024]{1,0:T(1,128)} %bitcast.133, bf16[1024,1024]{1,0:T(8,128)(2,1)} %wq_ref.1, bf16[1024,2048]{1,0:T(8,128)(2,1)} %wv_ref.1), custom_call_target="tpu_custom_call" | custom-call | flops 4831838208 | bytes 14000000 | tf_op jit(solution)/shard_map/project/pallas_call | solution.py:81
  17.2 4.9 %collective-permute-done.mem_ref = bf16[768,1024]{1,0:T(8,128)(2,1)} collective-permute-done((bf16[768,1024]{1,0:T(8,128)(2,1)}, bf16[768,1024]{1,0:T(8,128)(2,1)}, u32[]{:S(2)}, u32[]{:S(2)}) %collective-permute-start) | collective-permute-done | bytes 1572896 | tf_op jit(solution)/shard_map/ppermute | solution.py:719
  22.2 18.1 %attend.1 = (bf16[1024,768]{1,0:T(8,128)(2,1)}, bf16[768,1024]{1,0:T(8,128)(2,1)}, bf16[768,1024]{1,0:T(8,128)(2,1)}, bf16[1536,1024]{1,0:T(8,128)(2,1)}, bf16[1...) custom-call(s32[1]{0:T(128)} %bitcast.5.has_ref, ...), custom_call_target="tpu_custom_call" | custom-call | flops 4000000000 | bytes 15000000 | tf_op jit(solution)/shard_map/attend/pallas_call | solution.py:344
  40.3 8.6 %all-to-all-start = ((f32[32,1,128]{2,1,0:T(1,128)}), f32[32,1,128]{2,1,0:T(1,128)}, u32[]{:S(2)}, u32[]{:S(2)}) async-start(f32[32,1,128]{2,1,0:T(1,128)} %bitcast.132), calls=%async_computation | async-start | bytes 32768 | tf_op jit(solution)/shard_map/all_to_all | solution.py:729
  48.9 6.9 %all-to-all-done = f32[32,1,128]{2,1,0:T(1,128)} async-done(((f32[32,1,128]{2,1,0:T(1,128)}), f32[32,1,128]{2,1,0:T(1,128)}, u32[]{:S(2)}, u32[]{:S(2)}) %all-to-all-start) | async-done | bytes 16416 | tf_op jit(solution)/shard_map/all_to_all | solution.py:729
  55.7 8.8 %cotangents.1 = (bf16[768,1024]{1,0:T(8,128)(2,1)}, bf16[1024,512]{1,0:T(8,128)(2,1)}, bf16[1024,512]{1,0:T(8,128)(2,1)}, bf16[1024,128]{1,0:T(8,128)(2,1)}) custom-call(s32[1]{0:T(128)} %bitcast.4.me_ref, f32[32,128]{1,0:T(8,128)} %bitcast.10.told_ref, f32[5,8,128]{2,1,0:T(8,128)} %get-tuple-element.33.stats_ref, s32[6,128]{1,0:T(8,128)} %rewards_ref.3, ...), custom_call_target="tpu_custom_call" | custom-call | flops 4000000000 | bytes 12000000 | tf_op jit(solution)/shard_map/cotangents/pallas_call | solution.py:447
  64.5 12.5 %heads_backward.3 = bf16[1024,1536]{1,0:T(8,128)(2,1)} custom-call(s32[1]{0:T(128)} %bitcast.12.first_ref, bf16[768,1024]{1,0:T(8,128)(2,1)} %get-tuple-element.36.cot_ref, bf16[1536,1024]{1,0:T(8,128)(2,1)} %get-tuple-element.37.probs_ref, bf16[768,3072]{1,0:T(8,128)(2,1)} %get-tuple-element.31.q_ref.kc_ref.vc_ref, ...), custom_call_target="tpu_custom_call" | custom-call | flops 5000000000 | bytes 14000000 | tf_op jit(solution)/shard_map/heads_backward/pallas_call | solution.py:554
  77.0 0.8 collective-permute-start.1
  77.8 0.1 collective-permute-start.2
  77.9 0.6 pad_add_fusion.place_ref
  78.5 12.6 %heads_backward.2 = bf16[1024,1536]{1,0:T(8,128)(2,1)} custom-call(s32[1]{0:T(128)} %bitcast.3.first_ref, bf16[768,1024]{1,0:T(8,128)(2,1)} %get-tuple-element.36.cot_ref, bf16[1536,1024]{1,0:T(8,128)(2,1)} %get-tuple-element.37.probs_ref, bf16[768,3072]{1,0:T(8,128)(2,1)} %get-tuple-element.31.q_ref.kc_ref.vc_ref, ...), custom_call_target="tpu_custom_call" | custom-call | flops 5000000000 | bytes 14000000 | tf_op jit(solution)/shard_map/heads_backward/pallas_call | solution.py:554
  91.1 0.0 collective-permute-done.2
  91.1 0.0 collective-permute-done.1
  91.2 7.1 %pair_sum.1 = (bf16[4,4,16,768]{3,2,1,0:T(8,128)(2,1)}, bf16[4,4,16,768]{3,2,1,0:T(8,128)(2,1)}, bf16[4,4,16,768]{3,2,1,0:T(8,128)(2,1)}, bf16[4,4,16,768]{3,2,1...) custom-call(s32[3]{0:T(128)} %pad_add_fusion.place_ref, ...), custom_call_target="tpu_custom_call" | custom-call | tf_op jit(solution)/shard_map/pair_sum/pallas_call | solution.py:635
  98.2 3.8 %collective-permute-start.8 = (bf16[4,4,16,640]{3,2,1,0:T(8,128)(2,1)}, bf16[4,4,16,640]{3,2,1,0:T(8,128)(2,1)S(1)}, u32[]{:S(2)}, u32[]{:S(2)}) collective-permute-start(bf16[4,4,16,640]{3,2,1,0:T(8,128)(2,1)} %get-tuple-element.52), channel_id=1, source_target_pairs={{0,96},{32,0},{64,32},{96,64},{1,97},{33,1},{65,33},{97,65},{2,98}... | collective-permute-start | bytes 983048 | tf_op jit(solution)/shard_map/ppermute | solution.py:661
  102.1 0.0 collective-permute-start.7
  102.1 1.3 collective-permute-start.6
  103.4 0.9 collective-permute-start.5
  104.3 0.6 collective-permute-start.4
  104.8 11.2 %collective-permute-done.8 = bf16[4,4,16,640]{3,2,1,0:T(8,128)(2,1)S(1)} collective-permute-done((bf16[4,4,16,640]{3,2,1,0:T(8,128)(2,1)}, bf16[4,4,16,640]{3,2,1,0:T(8,128)(2,1)S(1)}, u32[]{:S(2)}, u32[]{:S(2)}) %collective-permute-start.8) | collective-permute-done | bytes 327712 | tf_op jit(solution)/shard_map/ppermute | solution.py:661
  116.0 0.7 collective-permute-start.3
  116.8 2.3 %collective-permute-done.7 = bf16[4,4,16,640]{3,2,1,0:T(8,128)(2,1)S(1)} collective-permute-done((bf16[4,4,16,640]{3,2,1,0:T(8,128)(2,1)}, bf16[4,4,16,640]{3,2,1,0:T(8,128)(2,1)S(1)}, u32[]{:S(2)}, u32[]{:S(2)}) %collective-permute-start.7) | collective-permute-done | bytes 327712 | tf_op jit(solution)/shard_map/ppermute | solution.py:661
  119.1 0.7 collective-permute-start.14
  119.8 0.0 collective-permute-done.6
  119.8 0.7 collective-permute-start.13
  120.5 1.1 convert_add_fusion.2
  121.7 0.0 collective-permute-done.5
  121.7 1.0 collective-permute-start.12
  122.8 0.0 collective-permute-done.4
  122.8 4.4 %collective-permute-done.3 = bf16[4,4,16,768]{3,2,1,0:T(8,128)(2,1)S(1)} collective-permute-done((bf16[4,4,16,768]{3,2,1,0:T(8,128)(2,1)}, bf16[4,4,16,768]{3,2,1,0:T(8,128)(2,1)S(1)}, u32[]{:S(2)}, u32[]{:S(2)}) %collective-permute-start.3) | collective-permute-done | bytes 393248 | tf_op jit(solution)/shard_map/ppermute | solution.py:661
  127.1 0.2 convert_add_fusion.1
  127.4 0.8 collective-permute-start.11
  128.2 0.8 collective-permute-start.10
  129.1 0.0 collective-permute-done.14
  129.1 1.0 collective-permute-start.9
  130.1 0.9 collective-permute-done.13
  131.0 6.5 %collective-permute-done.12 = bf16[4,4,16,768]{3,2,1,0:T(8,128)(2,1)S(1)} collective-permute-done((bf16[4,4,16,768]{3,2,1,0:T(8,128)(2,1)S(1)}, bf16[4,4,16,768]{3,2,1,0:T(8,128)(2,1)S(1)}, u32[]{:S(2)}, u32[]{:S(2)}) %collective-permute-start.12) | collective-permute-done | bytes 393248 | tf_op jit(solution)/shard_map/ppermute | solution.py:661
  137.6 0.2 convert_add_fusion
  137.8 0.8 collective-permute-start.17
  138.6 0.7 collective-permute-start.16
  139.3 1.4 collective-permute-done.11
  140.7 0.8 collective-permute-start.15
  141.5 3.0 %collective-permute-done.10 = bf16[4,16,1408]{2,1,0:T(8,128)(2,1)S(1)} collective-permute-done((bf16[4,16,1408]{2,1,0:T(8,128)(2,1)S(1)}, bf16[4,16,1408]{2,1,0:T(8,128)(2,1)S(1)}, u32[]{:S(2)}, u32[]{:S(2)}) %collective-permute-start.10) | collective-permute-done | bytes 180256 | tf_op jit(solution)/shard_map/ppermute | solution.py:661
  144.5 0.5 collective-permute-done.9
  145.0 0.1 convert_add_fusion.3
  145.1 0.8 collective-permute-start.20
  145.9 0.7 collective-permute-start.19
  146.6 0.0 collective-permute-done.17
  146.7 0.9 collective-permute-start.18
  147.5 0.0 collective-permute-done.16
  147.5 0.0 collective-permute-done.15
  147.6 0.7 collective-permute-done.20
  148.3 1.4 collective-permute-done.19
  149.8 1.5 collective-permute-done.18
  151.2 5.3 %collective-permute-start.21 = (f32[8,640]{1,0:T(8,128)S(1)}, f32[8,640]{1,0:T(8,128)S(1)}, u32[]{:S(2)}, u32[]{:S(2)}) collective-permute-start(f32[8,640]{1,0:T(8,128)S(1)} %dynamic-slice_bitcast_fusion), channel_id=1, source_target_pairs={{0,1},{1,0},{2,3},{3,2},{4,5},{5,4},{6,7},{7,6},{8,9},{9,8},{10,11... | collective-permute-start | bytes 61448 | tf_op jit(solution)/shard_map/ppermute | solution.py:655
  156.5 0.7 pad_maximum_fusion
  157.2 3.3 %all-to-all-start.1 = ((bf16[8,8,1536]{2,1,0:T(8,128)(2,1)}), bf16[8,8,1536]{2,1,0:T(8,128)(2,1)S(1)}, u32[]{:S(2)}, u32[]{:S(2)}) async-start(bf16[8,8,1536]{2,1,0:T(8,128)(2,1)} %pad_maximum_fusion), calls=%async_computation.1 | async-start | bytes 393216 | tf_op jit(solution)/shard_map/all_to_all | solution.py:688
  160.6 5.8 %all-to-all-done.1 = bf16[8,8,1536]{2,1,0:T(8,128)(2,1)S(1)} async-done(((bf16[8,8,1536]{2,1,0:T(8,128)(2,1)}), bf16[8,8,1536]{2,1,0:T(8,128)(2,1)S(1)}, u32[]{:S(2)}, u32[]{:S(2)}) %all-to-all-start.1) | async-done | bytes 196640 | tf_op jit(solution)/shard_map/all_to_all | solution.py:688
  166.6 0.6 multiply_reduce_fusion
  167.9 15.4 %all_to_all.22 = f32[128,1,128]{2,1,0:T(1,128)S(1)} all-to-all(f32[128,1,128]{2,1,0:T(1,128)S(1)} %broadcast_in_dim.3), channel_id=1, replica_groups=mesh['z'=4,'y'=4,'x'=4,'c'=2] {'z','y','x','c'}, dimensions={0} | all-to-all | bytes 131072 | tf_op jit(solution)/shard_map/all_to_all | solution.py:749
  183.3 0.6 reduce_sum.29
  184.6 0.7 broadcast_multiply_fusion
  (31 shorter events, 0.4 us)
Async XLA Ops:
  0.0 22.2 %collective-permute-start = (bf16[768,1024]{1,0:T(8,128)(2,1)}, bf16[768,1024]{1,0:T(8,128)(2,1)}, u32[]{:S(2)}, u32[]{:S(2)}) collective-permute-start(bf16[768,1024]{1,0:T(8,128)(2,1)} %bitcast.119), channel_id=1, source_target_pairs={{0,1},{1,2},{2,3},{3,4},{4,5},{5,6},{6,7},{7,8},{8,9},{9,10},{10,1... | collective-permute-start | bytes 4718600 | tf_op jit(solution)/shard_map/ppermute | solution.py:719
  40.3 15.4 %all-to-all-start = ((f32[32,1,128]{2,1,0:T(1,128)}), f32[32,1,128]{2,1,0:T(1,128)}, u32[]{:S(2)}, u32[]{:S(2)}) async-start(f32[32,1,128]{2,1,0:T(1,128)} %bitcast.132), calls=%async_computation | async-start | bytes 32768 | tf_op jit(solution)/shard_map/all_to_all | solution.py:729
  77.0 14.1 %collective-permute-start.1 = (bf16[1024,1536]{1,0:T(8,128)(2,1)}, bf16[1024,1536]{1,0:T(8,128)(2,1)}, u32[]{:S(2)}, u32[]{:S(2)}) collective-permute-start(bf16[1024,1536]{1,0:T(8,128)(2,1)} %heads_backward.3), channel_id=1, source_target_pairs={{0,1},{1,0},{2,3},{3,2},{4,5},{5,4},{6,7},{7,6},{8,9},{9,8},{10,11... | collective-permute-start | bytes 9437192 | tf_op jit(solution)/shard_map/ppermute | solution.py:655
  77.8 13.3 %collective-permute-start.2 = (bf16[1024,512]{1,0:T(8,128)(2,1)}, bf16[1024,512]{1,0:T(8,128)(2,1)}, u32[]{:S(2)}, u32[]{:S(2)}) collective-permute-start(bf16[1024,512]{1,0:T(8,128)(2,1)} %get-tuple-element.43), channel_id=1, source_target_pairs={{0,1},{1,0},{2,3},{3,2},{4,5},{5,4},{6,7},{7,6},{8,9},{9,8},{10,11... | collective-permute-start | bytes 3145736 | tf_op jit(solution)/shard_map/ppermute | solution.py:655
  98.2 23.5 %copy-start.2 = (bf16[4,4,16,768]{3,2,1,0:T(8,128)(2,1)S(1)}, bf16[4,4,16,768]{3,2,1,0:T(8,128)(2,1)}, u32[]{:S(2)}) copy-start(bf16[4,4,16,768]{3,2,1,0:T(8,128)(2,1)} %get-tuple-element.54) | copy-start | bytes 1179652
  98.2 28.9 %copy-start.1 = (bf16[4,4,16,768]{3,2,1,0:T(8,128)(2,1)S(1)}, bf16[4,4,16,768]{3,2,1,0:T(8,128)(2,1)}, u32[]{:S(2)}) copy-start(bf16[4,4,16,768]{3,2,1,0:T(8,128)(2,1)} %get-tuple-element.45) | copy-start | bytes 1179652
  98.2 17.8 %collective-permute-start.8 = (bf16[4,4,16,640]{3,2,1,0:T(8,128)(2,1)}, bf16[4,4,16,640]{3,2,1,0:T(8,128)(2,1)S(1)}, u32[]{:S(2)}, u32[]{:S(2)}) collective-permute-start(bf16[4,4,16,640]{3,2,1,0:T(8,128)(2,1)} %get-tuple-element.52), channel_id=1, source_target_pairs={{0,96},{32,0},{64,32},{96,64},{1,97},{33,1},{65,33},{97,65},{2,98}... | collective-permute-start | bytes 983048 | tf_op jit(solution)/shard_map/ppermute | solution.py:661
  102.1 17.0 %collective-permute-start.7 = (bf16[4,4,16,640]{3,2,1,0:T(8,128)(2,1)}, bf16[4,4,16,640]{3,2,1,0:T(8,128)(2,1)S(1)}, u32[]{:S(2)}, u32[]{:S(2)}) collective-permute-start(bf16[4,4,16,640]{3,2,1,0:T(8,128)(2,1)} %get-tuple-element.51), channel_id=1, source_target_pairs={{0,32},{32,64},{64,96},{96,0},{1,33},{33,65},{65,97},{97,1},{2,34}... | collective-permute-start | bytes 983048 | tf_op jit(solution)/shard_map/ppermute | solution.py:661
  102.1 17.7 %collective-permute-start.6 = (bf16[4,4,16,640]{3,2,1,0:T(8,128)(2,1)}, bf16[4,4,16,640]{3,2,1,0:T(8,128)(2,1)S(1)}, u32[]{:S(2)}, u32[]{:S(2)}) collective-permute-start(bf16[4,4,16,640]{3,2,1,0:T(8,128)(2,1)} %get-tuple-element.50), channel_id=1, source_target_pairs={{0,64},{32,96},{64,0},{96,32},{1,65},{33,97},{65,1},{97,33},{2,66}... | collective-permute-start | bytes 983048 | tf_op jit(solution)/shard_map/ppermute | solution.py:661
  103.4 18.4 %collective-permute-start.5 = (bf16[4,4,16,768]{3,2,1,0:T(8,128)(2,1)}, bf16[4,4,16,768]{3,2,1,0:T(8,128)(2,1)S(1)}, u32[]{:S(2)}, u32[]{:S(2)}) collective-permute-start(bf16[4,4,16,768]{3,2,1,0:T(8,128)(2,1)} %get-tuple-element.48), channel_id=1, source_target_pairs={{0,6},{2,0},{4,2},{6,4},{1,7},{3,1},{5,3},{7,5},{8,14},{10,8},{12,... | collective-permute-start | bytes 1179656 | tf_op jit(solution)/shard_map/ppermute | solution.py:661
  104.3 18.5 %collective-permute-start.4 = (bf16[4,4,16,768]{3,2,1,0:T(8,128)(2,1)}, bf16[4,4,16,768]{3,2,1,0:T(8,128)(2,1)S(1)}, u32[]{:S(2)}, u32[]{:S(2)}) collective-permute-start(bf16[4,4,16,768]{3,2,1,0:T(8,128)(2,1)} %get-tuple-element.47), channel_id=1, source_target_pairs={{0,2},{2,4},{4,6},{6,0},{1,3},{3,5},{5,7},{7,1},{8,10},{10,12},{12... | collective-permute-start | bytes 1179656 | tf_op jit(solution)/shard_map/ppermute | solution.py:661
  116.0 11.1 %collective-permute-start.3 = (bf16[4,4,16,768]{3,2,1,0:T(8,128)(2,1)}, bf16[4,4,16,768]{3,2,1,0:T(8,128)(2,1)S(1)}, u32[]{:S(2)}, u32[]{:S(2)}) collective-permute-start(bf16[4,4,16,768]{3,2,1,0:T(8,128)(2,1)} %get-tuple-element.46), channel_id=1, source_target_pairs={{0,4},{2,6},{4,0},{6,2},{1,5},{3,7},{5,1},{7,3},{8,12},{10,14},{12... | collective-permute-start | bytes 1179656 | tf_op jit(solution)/shard_map/ppermute | solution.py:661
  119.1 10.0 %collective-permute-start.14 = (bf16[4,4,16,768]{3,2,1,0:T(8,128)(2,1)}, bf16[4,4,16,768]{3,2,1,0:T(8,128)(2,1)S(1)}, u32[]{:S(2)}, u32[]{:S(2)}) collective-permute-start(bf16[4,4,16,768]{3,2,1,0:T(8,128)(2,1)} %get-tuple-element.56), channel_id=1, source_target_pairs={{0,24},{8,0},{16,8},{24,16},{1,25},{9,1},{17,9},{25,17},{2,26},{10... | collective-permute-start | bytes 1179656 | tf_op jit(solution)/shard_map/ppermute | solution.py:661
  119.8 11.2 %collective-permute-start.13 = (bf16[4,4,16,768]{3,2,1,0:T(8,128)(2,1)}, bf16[4,4,16,768]{3,2,1,0:T(8,128)(2,1)S(1)}, u32[]{:S(2)}, u32[]{:S(2)}) collective-permute-start(bf16[4,4,16,768]{3,2,1,0:T(8,128)(2,1)} %get-tuple-element.55), channel_id=1, source_target_pairs={{0,8},{8,16},{16,24},{24,0},{1,9},{9,17},{17,25},{25,1},{2,10},{10... | collective-permute-start | bytes 1179656 | tf_op jit(solution)/shard_map/ppermute | solution.py:661
  121.7 15.8 %collective-permute-start.12 = (bf16[4,4,16,768]{3,2,1,0:T(8,128)(2,1)S(1)}, bf16[4,4,16,768]{3,2,1,0:T(8,128)(2,1)S(1)}, u32[]{:S(2)}, u32[]{:S(2)}) collective-permute-start(bf16[4,4,16,768]{3,2,1,0:T(8,128)(2,1)S(1)} %copy-done.2), channel_id=1, source_target_pairs={{0,16},{8,24},{16,0},{24,8},{1,17},{9,25},{17,1},{25,9},{2,18},{10... | collective-permute-start | bytes 1179656 | tf_op jit(solution)/shard_map/ppermute | solution.py:661
  127.1 10.4 %copy-start = (bf16[4,4,16,768]{3,2,1,0:T(8,128)(2,1)S(1)}, bf16[4,4,16,768]{3,2,1,0:T(8,128)(2,1)}, u32[]{:S(2)}) copy-start(bf16[4,4,16,768]{3,2,1,0:T(8,128)(2,1)} %get-tuple-element.53) | copy-start | bytes 1179652
  127.4 13.3 %collective-permute-start.11 = (bf16[4,16,1408]{2,1,0:T(8,128)(2,1)S(1)}, bf16[4,16,1408]{2,1,0:T(8,128)(2,1)S(1)}, u32[]{:S(2)}, u32[]{:S(2)}) collective-permute-start(bf16[4,16,1408]{2,1,0:T(8,128)(2,1)S(1)} %pad_maximum_fusion.3), channel_id=1, source_target_pairs={{0,24},{8,0},{16,8},{24,16},{1,25},{9,1},{17,9},{25,17},{2,26},{10... | collective-permute-start | bytes 540680 | tf_op jit(solution)/shard_map/ppermute | solution.py:661
  128.2 16.2 %collective-permute-start.10 = (bf16[4,16,1408]{2,1,0:T(8,128)(2,1)S(1)}, bf16[4,16,1408]{2,1,0:T(8,128)(2,1)S(1)}, u32[]{:S(2)}, u32[]{:S(2)}) collective-permute-start(bf16[4,16,1408]{2,1,0:T(8,128)(2,1)S(1)} %pad_maximum_fusion.2), channel_id=1, source_target_pairs={{0,8},{8,16},{16,24},{24,0},{1,9},{9,17},{17,25},{25,1},{2,10},{10... | collective-permute-start | bytes 540680 | tf_op jit(solution)/shard_map/ppermute | solution.py:661
  129.1 15.9 %collective-permute-start.9 = (bf16[4,16,1408]{2,1,0:T(8,128)(2,1)S(1)}, bf16[4,16,1408]{2,1,0:T(8,128)(2,1)S(1)}, u32[]{:S(2)}, u32[]{:S(2)}) collective-permute-start(bf16[4,16,1408]{2,1,0:T(8,128)(2,1)S(1)} %pad_maximum_fusion.1), channel_id=1, source_target_pairs={{0,16},{8,24},{16,0},{24,8},{1,17},{9,25},{17,1},{25,9},{2,18},{10... | collective-permute-start | bytes 540680 | tf_op jit(solution)/shard_map/ppermute | solution.py:661
  137.8 8.9 %collective-permute-start.17 = (bf16[4,16,768]{2,1,0:T(8,128)(2,1)S(1)}, bf16[4,16,768]{2,1,0:T(8,128)(2,1)S(1)}, u32[]{:S(2)}, u32[]{:S(2)}) collective-permute-start(bf16[4,16,768]{2,1,0:T(8,128)(2,1)S(1)} %get-tuple-element.58), channel_id=1, source_target_pairs={{0,6},{2,0},{4,2},{6,4},{1,7},{3,1},{5,3},{7,5},{8,14},{10,8},{12,... | collective-permute-start | bytes 294920 | tf_op jit(solution)/shard_map/ppermute | solution.py:661
  138.6 8.9 %collective-permute-start.16 = (bf16[4,16,768]{2,1,0:T(8,128)(2,1)S(1)}, bf16[4,16,768]{2,1,0:T(8,128)(2,1)S(1)}, u32[]{:S(2)}, u32[]{:S(2)}) collective-permute-start(bf16[4,16,768]{2,1,0:T(8,128)(2,1)S(1)} %get-tuple-element.59), channel_id=1, source_target_pairs={{0,2},{2,4},{4,6},{6,0},{1,3},{3,5},{5,7},{7,1},{8,10},{10,12},{12... | collective-permute-start | bytes 294920 | tf_op jit(solution)/shard_map/ppermute | solution.py:661
  140.7 6.8 %collective-permute-start.15 = (bf16[4,16,768]{2,1,0:T(8,128)(2,1)S(1)}, bf16[4,16,768]{2,1,0:T(8,128)(2,1)S(1)}, u32[]{:S(2)}, u32[]{:S(2)}) collective-permute-start(bf16[4,16,768]{2,1,0:T(8,128)(2,1)S(1)} %get-tuple-element.57), channel_id=1, source_target_pairs={{0,4},{2,6},{4,0},{6,2},{1,5},{3,7},{5,1},{7,3},{8,12},{10,14},{12... | collective-permute-start | bytes 294920 | tf_op jit(solution)/shard_map/ppermute | solution.py:661
  145.1 3.2 %collective-permute-start.20 = (bf16[16,640]{1,0:T(8,128)(2,1)S(1)}, bf16[16,640]{1,0:T(8,128)(2,1)S(1)}, u32[]{:S(2)}, u32[]{:S(2)}) collective-permute-start(bf16[16,640]{1,0:T(8,128)(2,1)S(1)} %get-tuple-element.69), channel_id=1, source_target_pairs={{0,6},{2,0},{4,2},{6,4},{1,7},{3,1},{5,3},{7,5},{8,14},{10,8},{12,... | collective-permute-start | bytes 61448 | tf_op jit(solution)/shard_map/ppermute | solution.py:661
  145.9 3.8 %collective-permute-start.19 = (bf16[16,640]{1,0:T(8,128)(2,1)S(1)}, bf16[16,640]{1,0:T(8,128)(2,1)S(1)}, u32[]{:S(2)}, u32[]{:S(2)}) collective-permute-start(bf16[16,640]{1,0:T(8,128)(2,1)S(1)} %get-tuple-element.70), channel_id=1, source_target_pairs={{0,2},{2,4},{4,6},{6,0},{1,3},{3,5},{5,7},{7,1},{8,10},{10,12},{12... | collective-permute-start | bytes 61448 | tf_op jit(solution)/shard_map/ppermute | solution.py:661
  146.7 4.6 %collective-permute-start.18 = (bf16[16,640]{1,0:T(8,128)(2,1)S(1)}, bf16[16,640]{1,0:T(8,128)(2,1)S(1)}, u32[]{:S(2)}, u32[]{:S(2)}) collective-permute-start(bf16[16,640]{1,0:T(8,128)(2,1)S(1)} %get-tuple-element.68), channel_id=1, source_target_pairs={{0,4},{2,6},{4,0},{6,2},{1,5},{3,7},{5,1},{7,3},{8,12},{10,14},{12... | collective-permute-start | bytes 61448 | tf_op jit(solution)/shard_map/ppermute | solution.py:661
  151.2 9.3 %collective-permute-start.21 = (f32[8,640]{1,0:T(8,128)S(1)}, f32[8,640]{1,0:T(8,128)S(1)}, u32[]{:S(2)}, u32[]{:S(2)}) collective-permute-start(f32[8,640]{1,0:T(8,128)S(1)} %dynamic-slice_bitcast_fusion), channel_id=1, source_target_pairs={{0,1},{1,0},{2,3},{3,2},{4,5},{5,4},{6,7},{7,6},{8,9},{9,8},{10,11... | collective-permute-start | bytes 61448 | tf_op jit(solution)/shard_map/ppermute | solution.py:655
  157.2 9.2 %all-to-all-start.1 = ((bf16[8,8,1536]{2,1,0:T(8,128)(2,1)}), bf16[8,8,1536]{2,1,0:T(8,128)(2,1)S(1)}, u32[]{:S(2)}, u32[]{:S(2)}) async-start(bf16[8,8,1536]{2,1,0:T(8,128)(2,1)} %pad_maximum_fusion), calls=%async_computation.1 | async-start | bytes 393216 | tf_op jit(solution)/shard_map/all_to_all | solution.py:688
where the time goes:
time: 186 us; the launch traced here: 185 us
  Pallas kernels  70.5 us (38%)
  waiting for transfers between devices  51.4 us (28%)
  starting transfers between devices  39.8 us (21%)
  blocking collectives  15.4 us (8%)
  other arithmetic  4.96 us (3%)
    ppermute x18, waiting for transfers between devices, hop_sum(): got = lax.ppermute(blocks[step].astype(bf16), axis, ring(4, step))  33.8 us
    pallas_call x2, Pallas kernels, heads_backward(): pl.pallas_call(heads_kernel, grid_spec=pltpu.PrefetchScalarGridSpec(num_s...  25.1 us
    pallas_call x1, Pallas kernels, attend(): pl.pallas_call(attend_kernel, grid=(4,), in_specs=in_specs, out_specs=out...  18.1 us
    ppermute x18, starting transfers between devices, hop_sum(): got = lax.ppermute(blocks[step].astype(bf16), axis, ring(4, step))  17.2 us
    all_to_all x1, blocking collectives, body(): grand_total = jnp.sum(lax.all_to_all(spread, EVERY, 0, 0, tiled=True))  15.4 us
    pallas_call x1, Pallas kernels, project(): pl.pallas_call(project_kernel, grid=(6,), in_specs=[full((ROWS, WIDTH)),...  11.4 us
    pallas_call x1, Pallas kernels, cotangents(): pl.pallas_call(cotangent_kernel, grid=(4,), in_specs=[pl.BlockSpec(memory...  8.77 us
    all_to_all x1, starting transfers between devices, body(): told = lax.all_to_all(told, TIME, 0, 0, tiled=True)  8.55 us
  transfers between devices with their start and end apart: 24, of which 14 were waited for; matrix products, arithmetic and copies ran while one was open for 2% of the time, Pallas kernels for 13%

commit v1 on v0

--- a/solution.py
+++ b/solution.py
@@ -68,13 +68,17 @@
             normed_ref[rows, :] = normed
             turned_ref[:, rows] = normed.T
 
+    def put(columns):
+        out_ref[0] = columns[:, :PAIR]
+        out_ref[1] = columns[:, PAIR:]
+
     @pl.when(step < 2)
     def _():
-        out_ref[...] = dot(normed_ref[...], wq_ref[...], 1, 0).astype(bf16)
+        put(dot(normed_ref[...], wq_ref[...], 1, 0).astype(bf16))
 
     @pl.when(step >= 2)
     def _():
-        out_ref[...] = dot(normed_ref[...], wkv_ref[...], 1, 0).astype(bf16)
+        put(dot(normed_ref[...], wkv_ref[...], 1, 0).astype(bf16))
 
 
 def project(states, gain, w_query, w_keyval):
@@ -88,11 +92,11 @@
             pl.BlockSpec((WIDTH, 512), lambda j: (0, jnp.maximum(j - 2, 0))),
         ],
         out_specs=[
-            pl.BlockSpec((ROWS, 512), lambda j: (0, j)),
+            pl.BlockSpec((2, ROWS, PAIR), lambda j: (j, 0, 0)),
             full((WIDTH, ROWS)),
         ],
         out_shape=[
-            jax.ShapeDtypeStruct((ROWS, 3 * WIDTH), bf16),
+            jax.ShapeDtypeStruct((12, ROWS, PAIR), bf16),
             jax.ShapeDtypeStruct((WIDTH, ROWS), bf16),
         ],
         scratch_shapes=[pltpu.VMEM((ROWS, WIDTH), bf16)],
@@ -306,9 +310,9 @@
         full((1, WIDTH)),
         pl.BlockSpec((WIDTH, PAIR), lambda g: (0, g)),
         pl.BlockSpec((WIDTH, PAIR), lambda g: (0, 4 + g)),
-        pl.BlockSpec((ROWS, PAIR), lambda g: (0, g)),
-        pl.BlockSpec((ROWS, PAIR), lambda g: (0, 4 + g)),
-        pl.BlockSpec((ROWS, PAIR), lambda g: (0, 8 + g)),
+        pl.BlockSpec((None, ROWS, PAIR), lambda g: (g, 0, 0)),
+        pl.BlockSpec((None, ROWS, PAIR), lambda g: (4 + g, 0, 0)),
+        pl.BlockSpec((None, ROWS, PAIR), lambda g: (8 + g, 0, 0)),
         full((8, 2 * LEN)),
         pl.BlockSpec((PAIR, WIDTH), lambda g: (g, 0)),
         pl.BlockSpec(memory_space=pl.ANY),
@@ -323,9 +327,9 @@
     ]
     out_specs = [
         pl.BlockSpec(memory_space=pl.ANY),
-        pl.BlockSpec((ROWS, PAIR), lambda g: (0, g)),
-        pl.BlockSpec((ROWS, PAIR), lambda g: (0, g)),
-        pl.BlockSpec((2 * ROWS, PAIR), lambda g: (0, g)),
+        pl.BlockSpec((None, ROWS, PAIR), lambda g: (g, 0, 0)),
+        pl.BlockSpec((None, ROWS, PAIR), lambda g: (g, 0, 0)),
+        pl.BlockSpec((None, 2 * ROWS, PAIR), lambda g: (g, 0, 0)),
         pl.BlockSpec((PAIR, ROWS), lambda g: (g, 0)),
         pl.BlockSpec(memory_space=pl.ANY),
         full((5, 8, LEN)),
@@ -333,9 +337,9 @@
     ]
     out_shape = [
         jax.ShapeDtypeStruct((WIDTH, ROWS), bf16),
-        jax.ShapeDtypeStruct((ROWS, WIDTH), bf16),
-        jax.ShapeDtypeStruct((ROWS, WIDTH), bf16),
-        jax.ShapeDtypeStruct((2 * ROWS, WIDTH), bf16),
+        jax.ShapeDtypeStruct((4, ROWS, PAIR), bf16),
+        jax.ShapeDtypeStruct((4, ROWS, PAIR), bf16),
+        jax.ShapeDtypeStruct((4, 2 * ROWS, PAIR), bf16),
         jax.ShapeDtypeStruct((WIDTH, ROWS), bf16),
         jax.ShapeDtypeStruct((ROWS, WIDTH), bf16),
         jax.ShapeDtypeStruct((5, 8, LEN), f32),
@@ -464,13 +468,13 @@
             pl.BlockSpec((PAIR, ROWS), lambda n: (n, 0)),
         ],
         out_specs=[
-            pl.BlockSpec((ROWS, PAIR), lambda n: (0, n)),
+            pl.BlockSpec((None, ROWS, PAIR), lambda n: (n, 0, 0)),
             pl.BlockSpec((PAIR, HALF), lambda n: (n, 0)),
             pl.BlockSpec((PAIR, HALF), lambda n: (n, 0)),
             full((WIDTH, ACTS)),
         ],
         out_shape=[
-            jax.ShapeDtypeStruct((ROWS, WIDTH), bf16),
+            jax.ShapeDtypeStruct((4, ROWS, PAIR), bf16),
             jax.ShapeDtypeStruct((WIDTH, HALF), bf16),
             jax.ShapeDtypeStruct((WIDTH, HALF), bf16),
             jax.ShapeDtypeStruct((WIDTH, ACTS), bf16),
@@ -557,13 +561,13 @@
             num_scalar_prefetch=1,
             grid=(2,),
             in_specs=[
-                pl.BlockSpec((ROWS, PAIR), lambda g, first: (0, first[0] + g)),
-                pl.BlockSpec((2 * ROWS, PAIR), lambda g, first: (0, first[0] + g)),
-                pl.BlockSpec((ROWS, PAIR), lambda g, first: (0, first[0] + g)),
-                pl.BlockSpec((ROWS, PAIR), lambda g, first: (0, first[0] + g)),
-                pl.BlockSpec((ROWS, PAIR), lambda g, first: (0, 4 + first[0] + g)),
-                pl.BlockSpec((ROWS, PAIR), lambda g, first: (0, first[0] + g)),
-                pl.BlockSpec((ROWS, PAIR), lambda g, first: (0, 8 + first[0] + g)),
+                pl.BlockSpec((None, ROWS, PAIR), lambda g, first: (first[0] + g, 0, 0)),
+                pl.BlockSpec((None, 2 * ROWS, PAIR), lambda g, first: (first[0] + g, 0, 0)),
+                pl.BlockSpec((None, ROWS, PAIR), lambda g, first: (first[0] + g, 0, 0)),
+                pl.BlockSpec((None, ROWS, PAIR), lambda g, first: (first[0] + g, 0, 0)),
+                pl.BlockSpec((None, ROWS, PAIR), lambda g, first: (4 + first[0] + g, 0, 0)),
+                pl.BlockSpec((None, ROWS, PAIR), lambda g, first: (first[0] + g, 0, 0)),
+                pl.BlockSpec((None, ROWS, PAIR), lambda g, first: (8 + first[0] + g, 0, 0)),
                 full((WIDTH, ROWS)),
                 full((WIDTH, ROWS)),
             ],

time: 186 us -> 186 us (level)
  no operation moved by 1% of the time
where the time goes in v1:
time: 186 us; the launch traced here: 185 us
  Pallas kernels  70.2 us (38%)
  waiting for transfers between devices  51.5 us (28%)
  starting transfers between devices  39.8 us (21%)
  blocking collectives  15.4 us (8%)
  other arithmetic  4.96 us (3%)
    ppermute x18, waiting for transfers between devices, hop_sum(): got = lax.ppermute(blocks[step].astype(bf16), axis, ring(4, step))  33.8 us
    pallas_call x2, Pallas kernels, heads_backward(): pl.pallas_call(heads_kernel, grid_spec=pltpu.PrefetchScalarGridSpec(num_s...  25 us
    pallas_call x1, Pallas kernels, attend(): pl.pallas_call(attend_kernel, grid=(4,), in_specs=in_specs, out_specs=out...  18 us
    ppermute x18, starting transfers between devices, hop_sum(): got = lax.ppermute(blocks[step].astype(bf16), axis, ring(4, step))  17.1 us
    all_to_all x1, blocking collectives, body(): grand_total = jnp.sum(lax.all_to_all(spread, EVERY, 0, 0, tiled=True))  15.4 us
    pallas_call x1, Pallas kernels, project(): pl.pallas_call(project_kernel, grid=(6,), in_specs=[full((ROWS, WIDTH)),...  11.4 us
    pallas_call x1, Pallas kernels, cotangents(): pl.pallas_call(cotangent_kernel, grid=(4,), in_specs=[pl.BlockSpec(memory...  8.71 us
    all_to_all x1, starting transfers between devices, body(): told = lax.all_to_all(told, TIME, 0, 0, tiled=True)  8.55 us
  transfers between devices with their start and end apart: 24, of which 14 were waited for; matrix products, arithmetic and copies ran while one was open for 2% of the time, Pallas kernels for 13%

profile of v1, /device:TPU:1, one launch (start us, length us, event | category | flops | bytes accessed | tf_op | source)
XLA Modules:
  0.0 185.0 jit_solution(16941007304067817139)
XLA Ops:
  0.0 4.5 %collective-permute-start = (bf16[768,1024]{1,0:T(8,128)(2,1)}, bf16[768,1024]{1,0:T(8,128)(2,1)}, u32[]{:S(2)}, u32[]{:S(2)}) collective-permute-start(bf16[768,1024]{1,0:T(8,128)(2,1)} %bitcast.119), channel_id=1, source_target_pairs={{0,1},{1,2},{2,3},{3,4},{4,5},{5,6},{6,7},{7,8},{8,9},{9,10},{10,1... | collective-permute-start | bytes 4718600 | tf_op jit(solution)/shard_map/ppermute | solution.py:723
  4.5 1.3 reshape.86.wvalue_ref
  5.8 11.4 %project.1 = (bf16[12,768,256]{2,1,0:T(8,128)(2,1)}, bf16[1024,768]{1,0:T(8,128)(2,1)}) custom-call(bf16[768,1024]{1,0:T(8,128)(2,1)} %bitcast.120, f32[1,1024]{1,0:T(1,128)} %bitcast.133, bf16[1024,1024]{1,0:T(8,128)(2,1)} %wq_ref.1, bf16[1024,2048]{1,0:T(8,128)(2,1)} %wv_ref.1), custom_call_target="tpu_custom_call" | custom-call | flops 4831838208 | bytes 14000000 | tf_op jit(solution)/shard_map/project/pallas_call | solution.py:85
  17.2 5.0 %collective-permute-done.mem_ref = bf16[768,1024]{1,0:T(8,128)(2,1)} collective-permute-done((bf16[768,1024]{1,0:T(8,128)(2,1)}, bf16[768,1024]{1,0:T(8,128)(2,1)}, u32[]{:S(2)}, u32[]{:S(2)}) %collective-permute-start) | collective-permute-done | bytes 1572896 | tf_op jit(solution)/shard_map/ppermute | solution.py:723
  22.2 18.0 %attend.1 = (bf16[1024,768]{1,0:T(8,128)(2,1)}, bf16[4,768,256]{2,1,0:T(8,128)(2,1)}, bf16[4,768,256]{2,1,0:T(8,128)(2,1)}, bf16[4,1536,256]{2,1,0:T(8,128)(2,1)...) custom-call(s32[1]{0:T(128)} %bitcast.5.has_ref, ...), custom_call_target="tpu_custom_call" | custom-call | flops 4000000000 | bytes 15000000 | tf_op jit(solution)/shard_map/attend/pallas_call | solution.py:348
  40.2 8.6 %all-to-all-start = ((f32[32,1,128]{2,1,0:T(1,128)}), f32[32,1,128]{2,1,0:T(1,128)}, u32[]{:S(2)}, u32[]{:S(2)}) async-start(f32[32,1,128]{2,1,0:T(1,128)} %bitcast.132), calls=%async_computation | async-start | bytes 32768 | tf_op jit(solution)/shard_map/all_to_all | solution.py:733
  48.8 6.9 %all-to-all-done = f32[32,1,128]{2,1,0:T(1,128)} async-done(((f32[32,1,128]{2,1,0:T(1,128)}), f32[32,1,128]{2,1,0:T(1,128)}, u32[]{:S(2)}, u32[]{:S(2)}) %all-to-all-start) | async-done | bytes 16416 | tf_op jit(solution)/shard_map/all_to_all | solution.py:733
  55.6 8.7 %cotangents.1 = (bf16[4,768,256]{2,1,0:T(8,128)(2,1)}, bf16[1024,512]{1,0:T(8,128)(2,1)}, bf16[1024,512]{1,0:T(8,128)(2,1)}, bf16[1024,128]{1,0:T(8,128)(2,1)}) custom-call(s32[1]{0:T(128)} %bitcast.4.me_ref, f32[32,128]{1,0:T(8,128)} %bitcast.10.told_ref, f32[5,8,128]{2,1,0:T(8,128)} %get-tuple-element.33.stats_ref, s32[6,128]{1,0:T(8,128)} %rewards_ref.3, ...), custom_call_target="tpu_custom_call" | custom-call | flops 4000000000 | bytes 12000000 | tf_op jit(solution)/shard_map/cotangents/pallas_call | solution.py:451
  64.3 12.4 %heads_backward.3 = bf16[1024,1536]{1,0:T(8,128)(2,1)} custom-call(s32[1]{0:T(128)} %bitcast.12.first_ref, bf16[4,768,256]{2,1,0:T(8,128)(2,1)} %get-tuple-element.36.cot_ref, bf16[4,1536,256]{2,1,0:T(8,128)(2,1)} %get-tuple-element.37.probs_ref, bf16[12,768,256]{2,1,0:T(8,128)(2,1)} %get-tuple-element.31.q_ref.kc_ref.vc_ref, ...), custom_call_target="tpu_custom_call" | custom-call | flops 5000000000 | bytes 14000000 | tf_op jit(solution)/shard_map/heads_backward/pallas_call | solution.py:558
  76.8 0.8 collective-permute-start.1
  77.6 0.1 collective-permute-start.2
  77.7 0.6 pad_add_fusion.place_ref
  78.3 12.6 %heads_backward.2 = bf16[1024,1536]{1,0:T(8,128)(2,1)} custom-call(s32[1]{0:T(128)} %bitcast.3.first_ref, bf16[4,768,256]{2,1,0:T(8,128)(2,1)} %get-tuple-element.36.cot_ref, bf16[4,1536,256]{2,1,0:T(8,128)(2,1)} %get-tuple-element.37.probs_ref, bf16[12,768,256]{2,1,0:T(8,128)(2,1)} %get-tuple-element.31.q_ref.kc_ref.vc_ref, ...), custom_call_target="tpu_custom_call" | custom-call | flops 5000000000 | bytes 14000000 | tf_op jit(solution)/shard_map/heads_backward/pallas_call | solution.py:558
  90.8 0.0 collective-permute-done.2
  90.8 0.0 collective-permute-done.1
  90.8 7.1 %pair_sum.1 = (bf16[4,4,16,768]{3,2,1,0:T(8,128)(2,1)}, bf16[4,4,16,768]{3,2,1,0:T(8,128)(2,1)}, bf16[4,4,16,768]{3,2,1,0:T(8,128)(2,1)}, bf16[4,4,16,768]{3,2,1...) custom-call(s32[3]{0:T(128)} %pad_add_fusion.place_ref, ...), custom_call_target="tpu_custom_call" | custom-call | tf_op jit(solution)/shard_map/pair_sum/pallas_call | solution.py:639
  97.9 3.8 %collective-permute-start.8 = (bf16[4,4,16,640]{3,2,1,0:T(8,128)(2,1)}, bf16[4,4,16,640]{3,2,1,0:T(8,128)(2,1)S(1)}, u32[]{:S(2)}, u32[]{:S(2)}) collective-permute-start(bf16[4,4,16,640]{3,2,1,0:T(8,128)(2,1)} %get-tuple-element.52), channel_id=1, source_target_pairs={{0,96},{32,0},{64,32},{96,64},{1,97},{33,1},{65,33},{97,65},{2,98}... | collective-permute-start | bytes 983048 | tf_op jit(solution)/shard_map/ppermute | solution.py:665
  101.8 0.0 collective-permute-start.7
  101.8 1.3 collective-permute-start.6
  103.0 0.9 collective-permute-start.5
  103.9 0.6 collective-permute-start.4
  104.5 11.2 %collective-permute-done.8 = bf16[4,4,16,640]{3,2,1,0:T(8,128)(2,1)S(1)} collective-permute-done((bf16[4,4,16,640]{3,2,1,0:T(8,128)(2,1)}, bf16[4,4,16,640]{3,2,1,0:T(8,128)(2,1)S(1)}, u32[]{:S(2)}, u32[]{:S(2)}) %collective-permute-start.8) | collective-permute-done | bytes 327712 | tf_op jit(solution)/shard_map/ppermute | solution.py:665
  115.7 0.7 collective-permute-start.3
  116.5 2.3 %collective-permute-done.7 = bf16[4,4,16,640]{3,2,1,0:T(8,128)(2,1)S(1)} collective-permute-done((bf16[4,4,16,640]{3,2,1,0:T(8,128)(2,1)}, bf16[4,4,16,640]{3,2,1,0:T(8,128)(2,1)S(1)}, u32[]{:S(2)}, u32[]{:S(2)}) %collective-permute-start.7) | collective-permute-done | bytes 327712 | tf_op jit(solution)/shard_map/ppermute | solution.py:665
  118.8 0.7 collective-permute-start.14
  119.5 0.0 collective-permute-done.6
  119.5 0.7 collective-permute-start.13
  120.2 1.1 convert_add_fusion.2
  121.4 0.0 collective-permute-done.5
  121.4 1.0 collective-permute-start.12
  122.5 0.0 collective-permute-done.4
  122.5 4.4 %collective-permute-done.3 = bf16[4,4,16,768]{3,2,1,0:T(8,128)(2,1)S(1)} collective-permute-done((bf16[4,4,16,768]{3,2,1,0:T(8,128)(2,1)}, bf16[4,4,16,768]{3,2,1,0:T(8,128)(2,1)S(1)}, u32[]{:S(2)}, u32[]{:S(2)}) %collective-permute-start.3) | collective-permute-done | bytes 393248 | tf_op jit(solution)/shard_map/ppermute | solution.py:665
  126.9 0.2 convert_add_fusion.1
  127.1 0.8 collective-permute-start.11
  127.9 0.8 collective-permute-start.10
  128.8 1.0 collective-permute-start.9
  129.8 1.0 collective-permute-done.13
  130.8 6.5 %collective-permute-done.12 = bf16[4,4,16,768]{3,2,1,0:T(8,128)(2,1)S(1)} collective-permute-done((bf16[4,4,16,768]{3,2,1,0:T(8,128)(2,1)S(1)}, bf16[4,4,16,768]{3,2,1,0:T(8,128)(2,1)S(1)}, u32[]{:S(2)}, u32[]{:S(2)}) %collective-permute-start.12) | collective-permute-done | bytes 393248 | tf_op jit(solution)/shard_map/ppermute | solution.py:665
  137.2 0.2 convert_add_fusion
  137.5 0.8 collective-permute-start.17
  138.3 0.7 collective-permute-start.16
  139.0 1.4 collective-permute-done.11
  140.4 0.7 collective-permute-start.15
  141.1 3.0 %collective-permute-done.10 = bf16[4,16,1408]{2,1,0:T(8,128)(2,1)S(1)} collective-permute-done((bf16[4,16,1408]{2,1,0:T(8,128)(2,1)S(1)}, bf16[4,16,1408]{2,1,0:T(8,128)(2,1)S(1)}, u32[]{:S(2)}, u32[]{:S(2)}) %collective-permute-start.10) | collective-permute-done | bytes 180256 | tf_op jit(solution)/shard_map/ppermute | solution.py:665
  144.2 0.5 collective-permute-done.9
  144.7 0.1 convert_add_fusion.3
  144.8 0.8 collective-permute-start.20
  145.6 0.7 collective-permute-start.19
  146.3 0.0 collective-permute-done.17
  146.3 0.9 collective-permute-start.18
  147.2 0.0 collective-permute-done.16
  147.2 0.0 collective-permute-done.15
  147.3 0.7 collective-permute-done.20
  148.0 1.5 collective-permute-done.19
  149.5 1.3 collective-permute-done.18
  150.8 5.4 %collective-permute-start.21 = (f32[8,640]{1,0:T(8,128)S(1)}, f32[8,640]{1,0:T(8,128)S(1)}, u32[]{:S(2)}, u32[]{:S(2)}) collective-permute-start(f32[8,640]{1,0:T(8,128)S(1)} %dynamic-slice_bitcast_fusion), channel_id=1, source_target_pairs={{0,1},{1,0},{2,3},{3,2},{4,5},{5,4},{6,7},{7,6},{8,9},{9,8},{10,11... | collective-permute-start | bytes 61448 | tf_op jit(solution)/shard_map/ppermute | solution.py:659
  156.2 0.7 pad_maximum_fusion
  156.9 3.3 %all-to-all-start.1 = ((bf16[8,8,1536]{2,1,0:T(8,128)(2,1)}), bf16[8,8,1536]{2,1,0:T(8,128)(2,1)S(1)}, u32[]{:S(2)}, u32[]{:S(2)}) async-start(bf16[8,8,1536]{2,1,0:T(8,128)(2,1)} %pad_maximum_fusion), calls=%async_computation.1 | async-start | bytes 393216 | tf_op jit(solution)/shard_map/all_to_all | solution.py:692
  160.3 0.0 collective-permute-done.21
  160.3 5.8 %all-to-all-done.1 = bf16[8,8,1536]{2,1,0:T(8,128)(2,1)S(1)} async-done(((bf16[8,8,1536]{2,1,0:T(8,128)(2,1)}), bf16[8,8,1536]{2,1,0:T(8,128)(2,1)S(1)}, u32[]{:S(2)}, u32[]{:S(2)}) %all-to-all-start.1) | async-done | bytes 196640 | tf_op jit(solution)/shard_map/all_to_all | solution.py:692
  166.3 0.6 multiply_reduce_fusion
  167.6 15.4 %all_to_all.22 = f32[128,1,128]{2,1,0:T(1,128)S(1)} all-to-all(f32[128,1,128]{2,1,0:T(1,128)S(1)} %broadcast_in_dim.3), channel_id=1, replica_groups=mesh['z'=4,'y'=4,'x'=4,'c'=2] {'z','y','x','c'}, dimensions={0} | all-to-all | bytes 131072 | tf_op jit(solution)/shard_map/all_to_all | solution.py:753
  183.0 0.6 reduce_sum.29
  184.3 0.7 broadcast_multiply_fusion
  (31 shorter events, 0.4 us)
Async XLA Ops:
  0.0 22.2 %collective-permute-start = (bf16[768,1024]{1,0:T(8,128)(2,1)}, bf16[768,1024]{1,0:T(8,128)(2,1)}, u32[]{:S(2)}, u32[]{:S(2)}) collective-permute-start(bf16[768,1024]{1,0:T(8,128)(2,1)} %bitcast.119), channel_id=1, source_target_pairs={{0,1},{1,2},{2,3},{3,4},{4,5},{5,6},{6,7},{7,8},{8,9},{9,10},{10,1... | collective-permute-start | bytes 4718600 | tf_op jit(solution)/shard_map/ppermute | solution.py:723
  40.2 15.4 %all-to-all-start = ((f32[32,1,128]{2,1,0:T(1,128)}), f32[32,1,128]{2,1,0:T(1,128)}, u32[]{:S(2)}, u32[]{:S(2)}) async-start(f32[32,1,128]{2,1,0:T(1,128)} %bitcast.132), calls=%async_computation | async-start | bytes 32768 | tf_op jit(solution)/shard_map/all_to_all | solution.py:733
  76.8 14.1 %collective-permute-start.1 = (bf16[1024,1536]{1,0:T(8,128)(2,1)}, bf16[1024,1536]{1,0:T(8,128)(2,1)}, u32[]{:S(2)}, u32[]{:S(2)}) collective-permute-start(bf16[1024,1536]{1,0:T(8,128)(2,1)} %heads_backward.3), channel_id=1, source_target_pairs={{0,1},{1,0},{2,3},{3,2},{4,5},{5,4},{6,7},{7,6},{8,9},{9,8},{10,11... | collective-permute-start | bytes 9437192 | tf_op jit(solution)/shard_map/ppermute | solution.py:659
  77.6 13.2 %collective-permute-start.2 = (bf16[1024,512]{1,0:T(8,128)(2,1)}, bf16[1024,512]{1,0:T(8,128)(2,1)}, u32[]{:S(2)}, u32[]{:S(2)}) collective-permute-start(bf16[1024,512]{1,0:T(8,128)(2,1)} %get-tuple-element.43), channel_id=1, source_target_pairs={{0,1},{1,0},{2,3},{3,2},{4,5},{5,4},{6,7},{7,6},{8,9},{9,8},{10,11... | collective-permute-start | bytes 3145736 | tf_op jit(solution)/shard_map/ppermute | solution.py:659
  97.9 23.5 %copy-start.2 = (bf16[4,4,16,768]{3,2,1,0:T(8,128)(2,1)S(1)}, bf16[4,4,16,768]{3,2,1,0:T(8,128)(2,1)}, u32[]{:S(2)}) copy-start(bf16[4,4,16,768]{3,2,1,0:T(8,128)(2,1)} %get-tuple-element.54) | copy-start | bytes 1179652
  97.9 28.9 %copy-start.1 = (bf16[4,4,16,768]{3,2,1,0:T(8,128)(2,1)S(1)}, bf16[4,4,16,768]{3,2,1,0:T(8,128)(2,1)}, u32[]{:S(2)}) copy-start(bf16[4,4,16,768]{3,2,1,0:T(8,128)(2,1)} %get-tuple-element.45) | copy-start | bytes 1179652
  97.9 17.8 %collective-permute-start.8 = (bf16[4,4,16,640]{3,2,1,0:T(8,128)(2,1)}, bf16[4,4,16,640]{3,2,1,0:T(8,128)(2,1)S(1)}, u32[]{:S(2)}, u32[]{:S(2)}) collective-permute-start(bf16[4,4,16,640]{3,2,1,0:T(8,128)(2,1)} %get-tuple-element.52), channel_id=1, source_target_pairs={{0,96},{32,0},{64,32},{96,64},{1,97},{33,1},{65,33},{97,65},{2,98}... | collective-permute-start | bytes 983048 | tf_op jit(solution)/shard_map/ppermute | solution.py:665
  101.8 17.0 %collective-permute-start.7 = (bf16[4,4,16,640]{3,2,1,0:T(8,128)(2,1)}, bf16[4,4,16,640]{3,2,1,0:T(8,128)(2,1)S(1)}, u32[]{:S(2)}, u32[]{:S(2)}) collective-permute-start(bf16[4,4,16,640]{3,2,1,0:T(8,128)(2,1)} %get-tuple-element.51), channel_id=1, source_target_pairs={{0,32},{32,64},{64,96},{96,0},{1,33},{33,65},{65,97},{97,1},{2,34}... | collective-permute-start | bytes 983048 | tf_op jit(solution)/shard_map/ppermute | solution.py:665
  101.8 17.7 %collective-permute-start.6 = (bf16[4,4,16,640]{3,2,1,0:T(8,128)(2,1)}, bf16[4,4,16,640]{3,2,1,0:T(8,128)(2,1)S(1)}, u32[]{:S(2)}, u32[]{:S(2)}) collective-permute-start(bf16[4,4,16,640]{3,2,1,0:T(8,128)(2,1)} %get-tuple-element.50), channel_id=1, source_target_pairs={{0,64},{32,96},{64,0},{96,32},{1,65},{33,97},{65,1},{97,33},{2,66}... | collective-permute-start | bytes 983048 | tf_op jit(solution)/shard_map/ppermute | solution.py:665
  103.0 18.4 %collective-permute-start.5 = (bf16[4,4,16,768]{3,2,1,0:T(8,128)(2,1)}, bf16[4,4,16,768]{3,2,1,0:T(8,128)(2,1)S(1)}, u32[]{:S(2)}, u32[]{:S(2)}) collective-permute-start(bf16[4,4,16,768]{3,2,1,0:T(8,128)(2,1)} %get-tuple-element.48), channel_id=1, source_target_pairs={{0,6},{2,0},{4,2},{6,4},{1,7},{3,1},{5,3},{7,5},{8,14},{10,8},{12,... | collective-permute-start | bytes 1179656 | tf_op jit(solution)/shard_map/ppermute | solution.py:665
  103.9 18.5 %collective-permute-start.4 = (bf16[4,4,16,768]{3,2,1,0:T(8,128)(2,1)}, bf16[4,4,16,768]{3,2,1,0:T(8,128)(2,1)S(1)}, u32[]{:S(2)}, u32[]{:S(2)}) collective-permute-start(bf16[4,4,16,768]{3,2,1,0:T(8,128)(2,1)} %get-tuple-element.47), channel_id=1, source_target_pairs={{0,2},{2,4},{4,6},{6,0},{1,3},{3,5},{5,7},{7,1},{8,10},{10,12},{12... | collective-permute-start | bytes 1179656 | tf_op jit(solution)/shard_map/ppermute | solution.py:665
  115.7 11.1 %collective-permute-start.3 = (bf16[4,4,16,768]{3,2,1,0:T(8,128)(2,1)}, bf16[4,4,16,768]{3,2,1,0:T(8,128)(2,1)S(1)}, u32[]{:S(2)}, u32[]{:S(2)}) collective-permute-start(bf16[4,4,16,768]{3,2,1,0:T(8,128)(2,1)} %get-tuple-element.46), channel_id=1, source_target_pairs={{0,4},{2,6},{4,0},{6,2},{1,5},{3,7},{5,1},{7,3},{8,12},{10,14},{12... | collective-permute-start | bytes 1179656 | tf_op jit(solution)/shard_map/ppermute | solution.py:665
  118.8 10.0 %collective-permute-start.14 = (bf16[4,4,16,768]{3,2,1,0:T(8,128)(2,1)}, bf16[4,4,16,768]{3,2,1,0:T(8,128)(2,1)S(1)}, u32[]{:S(2)}, u32[]{:S(2)}) collective-permute-start(bf16[4,4,16,768]{3,2,1,0:T(8,128)(2,1)} %get-tuple-element.56), channel_id=1, source_target_pairs={{0,24},{8,0},{16,8},{24,16},{1,25},{9,1},{17,9},{25,17},{2,26},{10... | collective-permute-start | bytes 1179656 | tf_op jit(solution)/shard_map/ppermute | solution.py:665
  119.5 11.3 %collective-permute-start.13 = (bf16[4,4,16,768]{3,2,1,0:T(8,128)(2,1)}, bf16[4,4,16,768]{3,2,1,0:T(8,128)(2,1)S(1)}, u32[]{:S(2)}, u32[]{:S(2)}) collective-permute-start(bf16[4,4,16,768]{3,2,1,0:T(8,128)(2,1)} %get-tuple-element.55), channel_id=1, source_target_pairs={{0,8},{8,16},{16,24},{24,0},{1,9},{9,17},{17,25},{25,1},{2,10},{10... | collective-permute-start | bytes 1179656 | tf_op jit(solution)/shard_map/ppermute | solution.py:665
  121.4 15.8 %collective-permute-start.12 = (bf16[4,4,16,768]{3,2,1,0:T(8,128)(2,1)S(1)}, bf16[4,4,16,768]{3,2,1,0:T(8,128)(2,1)S(1)}, u32[]{:S(2)}, u32[]{:S(2)}) collective-permute-start(bf16[4,4,16,768]{3,2,1,0:T(8,128)(2,1)S(1)} %copy-done.2), channel_id=1, source_target_pairs={{0,16},{8,24},{16,0},{24,8},{1,17},{9,25},{17,1},{25,9},{2,18},{10... | collective-permute-start | bytes 1179656 | tf_op jit(solution)/shard_map/ppermute | solution.py:665
  126.9 10.4 %copy-start = (bf16[4,4,16,768]{3,2,1,0:T(8,128)(2,1)S(1)}, bf16[4,4,16,768]{3,2,1,0:T(8,128)(2,1)}, u32[]{:S(2)}) copy-start(bf16[4,4,16,768]{3,2,1,0:T(8,128)(2,1)} %get-tuple-element.53) | copy-start | bytes 1179652
  127.1 13.3 %collective-permute-start.11 = (bf16[4,16,1408]{2,1,0:T(8,128)(2,1)S(1)}, bf16[4,16,1408]{2,1,0:T(8,128)(2,1)S(1)}, u32[]{:S(2)}, u32[]{:S(2)}) collective-permute-start(bf16[4,16,1408]{2,1,0:T(8,128)(2,1)S(1)} %pad_maximum_fusion.3), channel_id=1, source_target_pairs={{0,24},{8,0},{16,8},{24,16},{1,25},{9,1},{17,9},{25,17},{2,26},{10... | collective-permute-start | bytes 540680 | tf_op jit(solution)/shard_map/ppermute | solution.py:665
  127.9 16.2 %collective-permute-start.10 = (bf16[4,16,1408]{2,1,0:T(8,128)(2,1)S(1)}, bf16[4,16,1408]{2,1,0:T(8,128)(2,1)S(1)}, u32[]{:S(2)}, u32[]{:S(2)}) collective-permute-start(bf16[4,16,1408]{2,1,0:T(8,128)(2,1)S(1)} %pad_maximum_fusion.2), channel_id=1, source_target_pairs={{0,8},{8,16},{16,24},{24,0},{1,9},{9,17},{17,25},{25,1},{2,10},{10... | collective-permute-start | bytes 540680 | tf_op jit(solution)/shard_map/ppermute | solution.py:665
  128.8 15.9 %collective-permute-start.9 = (bf16[4,16,1408]{2,1,0:T(8,128)(2,1)S(1)}, bf16[4,16,1408]{2,1,0:T(8,128)(2,1)S(1)}, u32[]{:S(2)}, u32[]{:S(2)}) collective-permute-start(bf16[4,16,1408]{2,1,0:T(8,128)(2,1)S(1)} %pad_maximum_fusion.1), channel_id=1, source_target_pairs={{0,16},{8,24},{16,0},{24,8},{1,17},{9,25},{17,1},{25,9},{2,18},{10... | collective-permute-start | bytes 540680 | tf_op jit(solution)/shard_map/ppermute | solution.py:665
  137.5 8.9 %collective-permute-start.17 = (bf16[4,16,768]{2,1,0:T(8,128)(2,1)S(1)}, bf16[4,16,768]{2,1,0:T(8,128)(2,1)S(1)}, u32[]{:S(2)}, u32[]{:S(2)}) collective-permute-start(bf16[4,16,768]{2,1,0:T(8,128)(2,1)S(1)} %get-tuple-element.58), channel_id=1, source_target_pairs={{0,6},{2,0},{4,2},{6,4},{1,7},{3,1},{5,3},{7,5},{8,14},{10,8},{12,... | collective-permute-start | bytes 294920 | tf_op jit(solution)/shard_map/ppermute | solution.py:665
  138.3 8.9 %collective-permute-start.16 = (bf16[4,16,768]{2,1,0:T(8,128)(2,1)S(1)}, bf16[4,16,768]{2,1,0:T(8,128)(2,1)S(1)}, u32[]{:S(2)}, u32[]{:S(2)}) collective-permute-start(bf16[4,16,768]{2,1,0:T(8,128)(2,1)S(1)} %get-tuple-element.59), channel_id=1, source_target_pairs={{0,2},{2,4},{4,6},{6,0},{1,3},{3,5},{5,7},{7,1},{8,10},{10,12},{12... | collective-permute-start | bytes 294920 | tf_op jit(solution)/shard_map/ppermute | solution.py:665
  140.4 6.8 %collective-permute-start.15 = (bf16[4,16,768]{2,1,0:T(8,128)(2,1)S(1)}, bf16[4,16,768]{2,1,0:T(8,128)(2,1)S(1)}, u32[]{:S(2)}, u32[]{:S(2)}) collective-permute-start(bf16[4,16,768]{2,1,0:T(8,128)(2,1)S(1)} %get-tuple-element.57), channel_id=1, source_target_pairs={{0,4},{2,6},{4,0},{6,2},{1,5},{3,7},{5,1},{7,3},{8,12},{10,14},{12... | collective-permute-start | bytes 294920 | tf_op jit(solution)/shard_map/ppermute | solution.py:665
  144.8 3.2 %collective-permute-start.20 = (bf16[16,640]{1,0:T(8,128)(2,1)S(1)}, bf16[16,640]{1,0:T(8,128)(2,1)S(1)}, u32[]{:S(2)}, u32[]{:S(2)}) collective-permute-start(bf16[16,640]{1,0:T(8,128)(2,1)S(1)} %get-tuple-element.69), channel_id=1, source_target_pairs={{0,6},{2,0},{4,2},{6,4},{1,7},{3,1},{5,3},{7,5},{8,14},{10,8},{12,... | collective-permute-start | bytes 61448 | tf_op jit(solution)/shard_map/ppermute | solution.py:665
  145.6 3.8 %collective-permute-start.19 = (bf16[16,640]{1,0:T(8,128)(2,1)S(1)}, bf16[16,640]{1,0:T(8,128)(2,1)S(1)}, u32[]{:S(2)}, u32[]{:S(2)}) collective-permute-start(bf16[16,640]{1,0:T(8,128)(2,1)S(1)} %get-tuple-element.70), channel_id=1, source_target_pairs={{0,2},{2,4},{4,6},{6,0},{1,3},{3,5},{5,7},{7,1},{8,10},{10,12},{12... | collective-permute-start | bytes 61448 | tf_op jit(solution)/shard_map/ppermute | solution.py:665
  146.3 4.5 %collective-permute-start.18 = (bf16[16,640]{1,0:T(8,128)(2,1)S(1)}, bf16[16,640]{1,0:T(8,128)(2,1)S(1)}, u32[]{:S(2)}, u32[]{:S(2)}) collective-permute-start(bf16[16,640]{1,0:T(8,128)(2,1)S(1)} %get-tuple-element.68), channel_id=1, source_target_pairs={{0,4},{2,6},{4,0},{6,2},{1,5},{3,7},{5,1},{7,3},{8,12},{10,14},{12... | collective-permute-start | bytes 61448 | tf_op jit(solution)/shard_map/ppermute | solution.py:665
  150.8 9.4 %collective-permute-start.21 = (f32[8,640]{1,0:T(8,128)S(1)}, f32[8,640]{1,0:T(8,128)S(1)}, u32[]{:S(2)}, u32[]{:S(2)}) collective-permute-start(f32[8,640]{1,0:T(8,128)S(1)} %dynamic-slice_bitcast_fusion), channel_id=1, source_target_pairs={{0,1},{1,0},{2,3},{3,2},{4,5},{5,4},{6,7},{7,6},{8,9},{9,8},{10,11... | collective-permute-start | bytes 61448 | tf_op jit(solution)/shard_map/ppermute | solution.py:659
  156.9 9.2 %all-to-all-start.1 = ((bf16[8,8,1536]{2,1,0:T(8,128)(2,1)}), bf16[8,8,1536]{2,1,0:T(8,128)(2,1)S(1)}, u32[]{:S(2)}, u32[]{:S(2)}) async-start(bf16[8,8,1536]{2,1,0:T(8,128)(2,1)} %pad_maximum_fusion), calls=%async_computation.1 | async-start | bytes 393216 | tf_op jit(solution)/shard_map/all_to_all | solution.py:692
